TPU v7x, 512 devices: a whole 4x4x16 slice. The times are simulated.
512 devices in a mesh: leaf: 512 (over x, z, y, core).
Axes of the slice: x: 4, y: 4, z: 16, core: 2. Of those that a mesh axis runs over, the one named last changes fastest.
Arguments:
- right_sides: bfloat16 [64, 524288], P(None, 'leaf'), may hold values from -6 to 6
- leaf_inverse: bfloat16 [524288, 1024], P('leaf'), may hold values from -0.1875 to 0.1875
- leaf_basis: bfloat16 [524288, 256], P('leaf'), may hold values from -0.1875 to 0.1875
- transfer: bfloat16 [262144, 256], P('leaf'), may hold values from -0.25 to 0.25
- coupling: bfloat16 [262144, 256], P('leaf'), may hold values from -0.25 to 0.25
Outputs:
- solution: bfloat16 [64, 524288], P(None, 'leaf')
All inputs are finite; a program needn't handle non-finite values.
Results may differ from a plain program's by a relative error of at most 0.025.
Values may be sent and summed in bfloat16 or wider, within the bound.
No kernel may reach another device: no remote copies, remote signals or barrier semaphores. Data moves between devices by JAX's collectives and lax.ppermute only.
A program may use at most 64 MiB of HBM per device.

v0:
```python
import jax
import jax.numpy as jnp
from jax import lax
from jax.sharding import PartitionSpec as P


def from_partner(block, axis, bit):
    count = lax.axis_size(axis)
    route = []
    for low in range(count):
        high = low | 1 << bit
        if high != low and high < count:
            route += [(low, high), (high, low)]
    return lax.ppermute(block, axis, route)


def times_matrix(values, matrix):
    return jnp.dot(values, matrix, preferred_element_type=jnp.float32)


def times_transposed(values, matrix):
    return lax.dot_general(
        values, matrix, (((1,), (1,)), ((), ())), preferred_element_type=jnp.float32
    )


def body(right_sides, leaf_inverse, leaf_basis, transfer, coupling):
    levels = lax.axis_size("leaf").bit_length() - 1
    rank_width = leaf_basis.shape[1]
    own_map = transfer[:rank_width]
    other_map = transfer[rank_width:]
    from_other = coupling[:rank_width]
    from_own = coupling[rank_width:]
    current = times_matrix(right_sides, leaf_basis).astype(jnp.bfloat16)
    own_values = []
    far_values = []
    for tree_level in range(1, levels + 1):
        other = from_partner(current, "leaf", tree_level - 1)
        own_values.append(current)
        far_values.append(other)
        current = (times_matrix(current, own_map) + times_matrix(other, other_map)).astype(
            jnp.bfloat16
        )
    node_h = current
    for tree_level in range(levels, 0, -1):
        own_t = own_values[tree_level - 1]
        other_h, far_t = from_partner((node_h, own_t), "leaf", tree_level - 1)
        total = times_transposed(node_h, own_map) + times_transposed(other_h, other_map)
        total = total + times_matrix(far_t, from_other)
        total = total + times_matrix(own_t, from_own)
        node_h = total.astype(jnp.bfloat16)
    total = times_matrix(right_sides, leaf_inverse) + times_transposed(node_h, leaf_basis)
    return total.astype(jnp.bfloat16)


def solution(mesh):
    placed = (P(None, "leaf"), P("leaf", None), P("leaf", None), P("leaf", None), P("leaf", None))
    return jax.shard_map(
        body, mesh=mesh, in_specs=placed, out_specs=P(None, "leaf"), check_vma=False
    )
```

profile of v0, /device:TPU:1, one launch (start us, length us, event | category | flops | bytes accessed | tf_op | source)
XLA Modules:
  0.0 148.7 jit_solution(2031863985131379086)
XLA Ops:
  1.5 8.7 %collective-permute-start = (bf16[64,256]{1,0:T(8,128)(2,1)S(1)}, bf16[64,256]{1,0:T(8,128)(2,1)S(1)}, u32[]{:S(2)}, u32[]{:S(2)}) collective-permute-start(bf16[64,256]{1,0:T(8,128)(2,1)S(1)} %convolution_convert_fusion), channel_id=1, source_target_pairs={{0,1},{1,0},{2,3},{3,2},{4,5},{5,4},{6,7},{7,6},{8,9},{9,8},{10,11... | collective-permute-start | bytes 98312 | tf_op jit(solution)/shard_map/ppermute | solution.py:14
  13.0 1.9 %collective-permute-start.1 = (bf16[64,256]{1,0:T(8,128)(2,1)S(1)}, bf16[64,256]{1,0:T(8,128)(2,1)S(1)}, u32[]{:S(2)}, u32[]{:S(2)}) collective-permute-start(bf16[64,256]{1,0:T(8,128)(2,1)S(1)} %fusion.10), channel_id=1, source_target_pairs={{0,2},{2,0},{1,3},{3,1},{4,6},{6,4},{5,7},{7,5},{8,10},{10,8},{9,1... | collective-permute-start | bytes 98312 | tf_op jit(solution)/shard_map/ppermute | solution.py:14
  15.2 2.4 %collective-permute-done.1 = bf16[64,256]{1,0:T(8,128)(2,1)S(1)} collective-permute-done((bf16[64,256]{1,0:T(8,128)(2,1)S(1)}, bf16[64,256]{1,0:T(8,128)(2,1)S(1)}, u32[]{:S(2)}, u32[]{:S(2)}) %collective-permute-start.1) | collective-permute-done | bytes 32800 | tf_op jit(solution)/shard_map/ppermute | solution.py:14
  17.8 1.9 %collective-permute-start.2 = (bf16[64,256]{1,0:T(8,128)(2,1)S(1)}, bf16[64,256]{1,0:T(8,128)(2,1)S(1)}, u32[]{:S(2)}, u32[]{:S(2)}) collective-permute-start(bf16[64,256]{1,0:T(8,128)(2,1)S(1)} %fusion.11), channel_id=1, source_target_pairs={{0,4},{4,0},{1,5},{5,1},{2,6},{6,2},{3,7},{7,3},{8,12},{12,8},{9,1... | collective-permute-start | bytes 98312 | tf_op jit(solution)/shard_map/ppermute | solution.py:14
  20.0 3.9 %collective-permute-done.2 = bf16[64,256]{1,0:T(8,128)(2,1)S(1)} collective-permute-done((bf16[64,256]{1,0:T(8,128)(2,1)S(1)}, bf16[64,256]{1,0:T(8,128)(2,1)S(1)}, u32[]{:S(2)}, u32[]{:S(2)}) %collective-permute-start.2) | collective-permute-done | bytes 32800 | tf_op jit(solution)/shard_map/ppermute | solution.py:14
  24.1 1.9 %collective-permute-start.3 = (bf16[64,256]{1,0:T(8,128)(2,1)S(1)}, bf16[64,256]{1,0:T(8,128)(2,1)S(1)}, u32[]{:S(2)}, u32[]{:S(2)}) collective-permute-start(bf16[64,256]{1,0:T(8,128)(2,1)S(1)} %fusion.12), channel_id=1, source_target_pairs={{0,8},{8,0},{1,9},{9,1},{2,10},{10,2},{3,11},{11,3},{4,12},{12,4},... | collective-permute-start | bytes 98312 | tf_op jit(solution)/shard_map/ppermute | solution.py:14
  26.3 2.4 %collective-permute-done.3 = bf16[64,256]{1,0:T(8,128)(2,1)S(1)} collective-permute-done((bf16[64,256]{1,0:T(8,128)(2,1)S(1)}, bf16[64,256]{1,0:T(8,128)(2,1)S(1)}, u32[]{:S(2)}, u32[]{:S(2)}) %collective-permute-start.3) | collective-permute-done | bytes 32800 | tf_op jit(solution)/shard_map/ppermute | solution.py:14
  28.9 1.9 %collective-permute-start.4 = (bf16[64,256]{1,0:T(8,128)(2,1)S(1)}, bf16[64,256]{1,0:T(8,128)(2,1)S(1)}, u32[]{:S(2)}, u32[]{:S(2)}) collective-permute-start(bf16[64,256]{1,0:T(8,128)(2,1)S(1)} %fusion.13), channel_id=1, source_target_pairs={{0,16},{16,0},{1,17},{17,1},{2,18},{18,2},{3,19},{19,3},{4,20},{20... | collective-permute-start | bytes 98312 | tf_op jit(solution)/shard_map/ppermute | solution.py:14
  31.1 3.4 %collective-permute-done.4 = bf16[64,256]{1,0:T(8,128)(2,1)S(1)} collective-permute-done((bf16[64,256]{1,0:T(8,128)(2,1)S(1)}, bf16[64,256]{1,0:T(8,128)(2,1)S(1)}, u32[]{:S(2)}, u32[]{:S(2)}) %collective-permute-start.4) | collective-permute-done | bytes 32800 | tf_op jit(solution)/shard_map/ppermute | solution.py:14
  34.9 4.2 %collective-permute-start.5 = (bf16[64,256]{1,0:T(8,128)(2,1)S(1)}, bf16[64,256]{1,0:T(8,128)(2,1)S(1)}, u32[]{:S(2)}, u32[]{:S(2)}) collective-permute-start(bf16[64,256]{1,0:T(8,128)(2,1)S(1)} %fusion.14), channel_id=1, source_target_pairs={{0,32},{32,0},{1,33},{33,1},{2,34},{34,2},{3,35},{35,3},{4,36},{36... | collective-permute-start | bytes 98312 | tf_op jit(solution)/shard_map/ppermute | solution.py:14
  39.2 4.9 %collective-permute-done.5 = bf16[64,256]{1,0:T(8,128)(2,1)S(1)} collective-permute-done((bf16[64,256]{1,0:T(8,128)(2,1)S(1)}, bf16[64,256]{1,0:T(8,128)(2,1)S(1)}, u32[]{:S(2)}, u32[]{:S(2)}) %collective-permute-start.5) | collective-permute-done | bytes 32800 | tf_op jit(solution)/shard_map/ppermute | solution.py:14
  44.4 9.3 %collective-permute-start.6 = (bf16[64,256]{1,0:T(8,128)(2,1)S(1)}, bf16[64,256]{1,0:T(8,128)(2,1)S(1)}, u32[]{:S(2)}, u32[]{:S(2)}) collective-permute-start(bf16[64,256]{1,0:T(8,128)(2,1)S(1)} %fusion.15), channel_id=1, source_target_pairs={{0,64},{64,0},{1,65},{65,1},{2,66},{66,2},{3,67},{67,3},{4,68},{68... | collective-permute-start | bytes 98312 | tf_op jit(solution)/shard_map/ppermute | solution.py:14
  53.9 3.9 %collective-permute-done.6 = bf16[64,256]{1,0:T(8,128)(2,1)S(1)} collective-permute-done((bf16[64,256]{1,0:T(8,128)(2,1)S(1)}, bf16[64,256]{1,0:T(8,128)(2,1)S(1)}, u32[]{:S(2)}, u32[]{:S(2)}) %collective-permute-start.6) | collective-permute-done | bytes 32800 | tf_op jit(solution)/shard_map/ppermute | solution.py:14
  58.1 1.9 %collective-permute-start.7 = (bf16[64,256]{1,0:T(8,128)(2,1)S(1)}, bf16[64,256]{1,0:T(8,128)(2,1)S(1)}, u32[]{:S(2)}, u32[]{:S(2)}) collective-permute-start(bf16[64,256]{1,0:T(8,128)(2,1)S(1)} %fusion.16), channel_id=1, source_target_pairs={{0,128},{128,0},{1,129},{129,1},{2,130},{130,2},{3,131},{131,3},{4... | collective-permute-start | bytes 98312 | tf_op jit(solution)/shard_map/ppermute | solution.py:14
  60.2 2.9 %collective-permute-done.7 = bf16[64,256]{1,0:T(8,128)(2,1)S(1)} collective-permute-done((bf16[64,256]{1,0:T(8,128)(2,1)S(1)}, bf16[64,256]{1,0:T(8,128)(2,1)S(1)}, u32[]{:S(2)}, u32[]{:S(2)}) %collective-permute-start.7) | collective-permute-done | bytes 32800 | tf_op jit(solution)/shard_map/ppermute | solution.py:14
  63.4 1.9 %collective-permute-start.8 = (bf16[64,256]{1,0:T(8,128)(2,1)S(1)}, bf16[64,256]{1,0:T(8,128)(2,1)S(1)}, u32[]{:S(2)}, u32[]{:S(2)}) collective-permute-start(bf16[64,256]{1,0:T(8,128)(2,1)S(1)} %fusion.17), channel_id=1, source_target_pairs={{0,256},{256,0},{1,257},{257,1},{2,258},{258,2},{3,259},{259,3},{4... | collective-permute-start | bytes 98312 | tf_op jit(solution)/shard_map/ppermute | solution.py:14
  65.5 4.3 %collective-permute-done.8 = bf16[64,256]{1,0:T(8,128)(2,1)S(1)} collective-permute-done((bf16[64,256]{1,0:T(8,128)(2,1)S(1)}, bf16[64,256]{1,0:T(8,128)(2,1)S(1)}, u32[]{:S(2)}, u32[]{:S(2)}) %collective-permute-start.8) | collective-permute-done | bytes 32800 | tf_op jit(solution)/shard_map/ppermute | solution.py:14
  69.9 1.9 %collective-permute-start.9 = (bf16[64,256]{1,0:T(8,128)(2,1)S(1)}, bf16[64,256]{1,0:T(8,128)(2,1)S(1)}, u32[]{:S(2)}, u32[]{:S(2)}) collective-permute-start(bf16[64,256]{1,0:T(8,128)(2,1)S(1)} %fusion.18), channel_id=1, source_target_pairs={{0,256},{256,0},{1,257},{257,1},{2,258},{258,2},{3,259},{259,3},{4... | collective-permute-start | bytes 98312 | tf_op jit(solution)/shard_map/ppermute | solution.py:14
  72.0 4.1 %collective-permute-done.9 = bf16[64,256]{1,0:T(8,128)(2,1)S(1)} collective-permute-done((bf16[64,256]{1,0:T(8,128)(2,1)S(1)}, bf16[64,256]{1,0:T(8,128)(2,1)S(1)}, u32[]{:S(2)}, u32[]{:S(2)}) %collective-permute-start.9) | collective-permute-done | bytes 32800 | tf_op jit(solution)/shard_map/ppermute | solution.py:14
  78.5 2.6 %collective-permute-done.10 = bf16[64,256]{1,0:T(8,128)(2,1)S(1)} collective-permute-done((bf16[64,256]{1,0:T(8,128)(2,1)S(1)}, bf16[64,256]{1,0:T(8,128)(2,1)S(1)}, u32[]{:S(2)}, u32[]{:S(2)}) %collective-permute-start.10) | collective-permute-done | bytes 32800 | tf_op jit(solution)/shard_map/ppermute | solution.py:14
  81.4 9.5 %collective-permute-start.11 = (bf16[64,256]{1,0:T(8,128)(2,1)S(1)}, bf16[64,256]{1,0:T(8,128)(2,1)S(1)}, u32[]{:S(2)}, u32[]{:S(2)}) collective-permute-start(bf16[64,256]{1,0:T(8,128)(2,1)S(1)} %fusion.20), channel_id=1, source_target_pairs={{0,64},{64,0},{1,65},{65,1},{2,66},{66,2},{3,67},{67,3},{4,68},{68... | collective-permute-start | bytes 98312 | tf_op jit(solution)/shard_map/ppermute | solution.py:14
  91.0 3.7 %collective-permute-done.11 = bf16[64,256]{1,0:T(8,128)(2,1)S(1)} collective-permute-done((bf16[64,256]{1,0:T(8,128)(2,1)S(1)}, bf16[64,256]{1,0:T(8,128)(2,1)S(1)}, u32[]{:S(2)}, u32[]{:S(2)}) %collective-permute-start.11) | collective-permute-done | bytes 32800 | tf_op jit(solution)/shard_map/ppermute | solution.py:14
  95.1 4.2 %collective-permute-start.12 = (bf16[64,256]{1,0:T(8,128)(2,1)S(1)}, bf16[64,256]{1,0:T(8,128)(2,1)S(1)}, u32[]{:S(2)}, u32[]{:S(2)}) collective-permute-start(bf16[64,256]{1,0:T(8,128)(2,1)S(1)} %fusion.21), channel_id=1, source_target_pairs={{0,32},{32,0},{1,33},{33,1},{2,34},{34,2},{3,35},{35,3},{4,36},{36... | collective-permute-start | bytes 98312 | tf_op jit(solution)/shard_map/ppermute | solution.py:14
  99.5 5.0 %collective-permute-done.12 = bf16[64,256]{1,0:T(8,128)(2,1)S(1)} collective-permute-done((bf16[64,256]{1,0:T(8,128)(2,1)S(1)}, bf16[64,256]{1,0:T(8,128)(2,1)S(1)}, u32[]{:S(2)}, u32[]{:S(2)}) %collective-permute-start.12) | collective-permute-done | bytes 32800 | tf_op jit(solution)/shard_map/ppermute | solution.py:14
  104.8 1.9 %collective-permute-start.13 = (bf16[64,256]{1,0:T(8,128)(2,1)S(1)}, bf16[64,256]{1,0:T(8,128)(2,1)S(1)}, u32[]{:S(2)}, u32[]{:S(2)}) collective-permute-start(bf16[64,256]{1,0:T(8,128)(2,1)S(1)} %fusion.22), channel_id=1, source_target_pairs={{0,16},{16,0},{1,17},{17,1},{2,18},{18,2},{3,19},{19,3},{4,20},{20... | collective-permute-start | bytes 98312 | tf_op jit(solution)/shard_map/ppermute | solution.py:14
  106.9 3.5 %collective-permute-done.13 = bf16[64,256]{1,0:T(8,128)(2,1)S(1)} collective-permute-done((bf16[64,256]{1,0:T(8,128)(2,1)S(1)}, bf16[64,256]{1,0:T(8,128)(2,1)S(1)}, u32[]{:S(2)}, u32[]{:S(2)}) %collective-permute-start.13) | collective-permute-done | bytes 32800 | tf_op jit(solution)/shard_map/ppermute | solution.py:14
  110.7 1.9 %collective-permute-start.14 = (bf16[64,256]{1,0:T(8,128)(2,1)S(1)}, bf16[64,256]{1,0:T(8,128)(2,1)S(1)}, u32[]{:S(2)}, u32[]{:S(2)}) collective-permute-start(bf16[64,256]{1,0:T(8,128)(2,1)S(1)} %fusion.23), channel_id=1, source_target_pairs={{0,8},{8,0},{1,9},{9,1},{2,10},{10,2},{3,11},{11,3},{4,12},{12,4},... | collective-permute-start | bytes 98312 | tf_op jit(solution)/shard_map/ppermute | solution.py:14
  112.8 2.9 %collective-permute-done.14 = bf16[64,256]{1,0:T(8,128)(2,1)S(1)} collective-permute-done((bf16[64,256]{1,0:T(8,128)(2,1)S(1)}, bf16[64,256]{1,0:T(8,128)(2,1)S(1)}, u32[]{:S(2)}, u32[]{:S(2)}) %collective-permute-start.14) | collective-permute-done | bytes 32800 | tf_op jit(solution)/shard_map/ppermute | solution.py:14
  116.0 2.4 %collective-permute-start.15 = (bf16[64,256]{1,0:T(8,128)(2,1)S(1)}, bf16[64,256]{1,0:T(8,128)(2,1)S(1)}, u32[]{:S(2)}, u32[]{:S(2)}) collective-permute-start(bf16[64,256]{1,0:T(8,128)(2,1)S(1)} %fusion.24), channel_id=1, source_target_pairs={{0,4},{4,0},{1,5},{5,1},{2,6},{6,2},{3,7},{7,3},{8,12},{12,8},{9,1... | collective-permute-start | bytes 98312 | tf_op jit(solution)/shard_map/ppermute | solution.py:14
  118.6 3.6 %collective-permute-done.15 = bf16[64,256]{1,0:T(8,128)(2,1)S(1)} collective-permute-done((bf16[64,256]{1,0:T(8,128)(2,1)S(1)}, bf16[64,256]{1,0:T(8,128)(2,1)S(1)}, u32[]{:S(2)}, u32[]{:S(2)}) %collective-permute-start.15) | collective-permute-done | bytes 32800 | tf_op jit(solution)/shard_map/ppermute | solution.py:14
  124.6 2.6 %collective-permute-done.16 = bf16[64,256]{1,0:T(8,128)(2,1)S(1)} collective-permute-done((bf16[64,256]{1,0:T(8,128)(2,1)S(1)}, bf16[64,256]{1,0:T(8,128)(2,1)S(1)}, u32[]{:S(2)}, u32[]{:S(2)}) %collective-permute-start.16) | collective-permute-done | bytes 32800 | tf_op jit(solution)/shard_map/ppermute | solution.py:14
  127.5 19.1 %collective-permute-start.17 = (bf16[64,256]{1,0:T(8,128)(2,1)S(1)}, bf16[64,256]{1,0:T(8,128)(2,1)S(1)}, u32[]{:S(2)}, u32[]{:S(2)}) collective-permute-start(bf16[64,256]{1,0:T(8,128)(2,1)S(1)} %fusion.26), channel_id=1, source_target_pairs={{0,1},{1,0},{2,3},{3,2},{4,5},{5,4},{6,7},{7,6},{8,9},{9,8},{10,11... | collective-permute-start | bytes 98312 | tf_op jit(solution)/shard_map/ppermute | solution.py:14
  (68 shorter events, 17.5 us)
Async XLA Ops:
  0.0 11.3 %copy-start = (bf16[1024,1024]{1,0:T(8,128)(2,1)S(1)}, bf16[1024,1024]{1,0:T(8,128)(2,1)}, u32[]{:S(2)}) copy-start(bf16[1024,1024]{1,0:T(8,128)(2,1)} %param.6) | copy-start | bytes 6291460
  0.0 12.8 %copy-start.1 = (bf16[512,256]{1,0:T(8,128)(2,1)S(1)}, bf16[512,256]{1,0:T(8,128)(2,1)}, u32[]{:S(2)}) copy-start(bf16[512,256]{1,0:T(8,128)(2,1)} %param.8) | copy-start | bytes 786436
  0.0 12.7 %copy-start.2 = (bf16[512,256]{1,0:T(8,128)(2,1)S(1)}, bf16[512,256]{1,0:T(8,128)(2,1)}, u32[]{:S(2)}) copy-start(bf16[512,256]{1,0:T(8,128)(2,1)} %param.9) | copy-start | bytes 786436
  1.5 11.3 %collective-permute-start = (bf16[64,256]{1,0:T(8,128)(2,1)S(1)}, bf16[64,256]{1,0:T(8,128)(2,1)S(1)}, u32[]{:S(2)}, u32[]{:S(2)}) collective-permute-start(bf16[64,256]{1,0:T(8,128)(2,1)S(1)} %convolution_convert_fusion), channel_id=1, source_target_pairs={{0,1},{1,0},{2,3},{3,2},{4,5},{5,4},{6,7},{7,6},{8,9},{9,8},{10,11... | collective-permute-start | bytes 98312 | tf_op jit(solution)/shard_map/ppermute | solution.py:14
  13.0 4.7 %collective-permute-start.1 = (bf16[64,256]{1,0:T(8,128)(2,1)S(1)}, bf16[64,256]{1,0:T(8,128)(2,1)S(1)}, u32[]{:S(2)}, u32[]{:S(2)}) collective-permute-start(bf16[64,256]{1,0:T(8,128)(2,1)S(1)} %fusion.10), channel_id=1, source_target_pairs={{0,2},{2,0},{1,3},{3,1},{4,6},{6,4},{5,7},{7,5},{8,10},{10,8},{9,1... | collective-permute-start | bytes 98312 | tf_op jit(solution)/shard_map/ppermute | solution.py:14
  17.8 6.2 %collective-permute-start.2 = (bf16[64,256]{1,0:T(8,128)(2,1)S(1)}, bf16[64,256]{1,0:T(8,128)(2,1)S(1)}, u32[]{:S(2)}, u32[]{:S(2)}) collective-permute-start(bf16[64,256]{1,0:T(8,128)(2,1)S(1)} %fusion.11), channel_id=1, source_target_pairs={{0,4},{4,0},{1,5},{5,1},{2,6},{6,2},{3,7},{7,3},{8,12},{12,8},{9,1... | collective-permute-start | bytes 98312 | tf_op jit(solution)/shard_map/ppermute | solution.py:14
  24.1 4.7 %collective-permute-start.3 = (bf16[64,256]{1,0:T(8,128)(2,1)S(1)}, bf16[64,256]{1,0:T(8,128)(2,1)S(1)}, u32[]{:S(2)}, u32[]{:S(2)}) collective-permute-start(bf16[64,256]{1,0:T(8,128)(2,1)S(1)} %fusion.12), channel_id=1, source_target_pairs={{0,8},{8,0},{1,9},{9,1},{2,10},{10,2},{3,11},{11,3},{4,12},{12,4},... | collective-permute-start | bytes 98312 | tf_op jit(solution)/shard_map/ppermute | solution.py:14
  28.9 5.6 %collective-permute-start.4 = (bf16[64,256]{1,0:T(8,128)(2,1)S(1)}, bf16[64,256]{1,0:T(8,128)(2,1)S(1)}, u32[]{:S(2)}, u32[]{:S(2)}) collective-permute-start(bf16[64,256]{1,0:T(8,128)(2,1)S(1)} %fusion.13), channel_id=1, source_target_pairs={{0,16},{16,0},{1,17},{17,1},{2,18},{18,2},{3,19},{19,3},{4,20},{20... | collective-permute-start | bytes 98312 | tf_op jit(solution)/shard_map/ppermute | solution.py:14
  34.9 9.3 %collective-permute-start.5 = (bf16[64,256]{1,0:T(8,128)(2,1)S(1)}, bf16[64,256]{1,0:T(8,128)(2,1)S(1)}, u32[]{:S(2)}, u32[]{:S(2)}) collective-permute-start(bf16[64,256]{1,0:T(8,128)(2,1)S(1)} %fusion.14), channel_id=1, source_target_pairs={{0,32},{32,0},{1,33},{33,1},{2,34},{34,2},{3,35},{35,3},{4,36},{36... | collective-permute-start | bytes 98312 | tf_op jit(solution)/shard_map/ppermute | solution.py:14
  44.4 13.4 %collective-permute-start.6 = (bf16[64,256]{1,0:T(8,128)(2,1)S(1)}, bf16[64,256]{1,0:T(8,128)(2,1)S(1)}, u32[]{:S(2)}, u32[]{:S(2)}) collective-permute-start(bf16[64,256]{1,0:T(8,128)(2,1)S(1)} %fusion.15), channel_id=1, source_target_pairs={{0,64},{64,0},{1,65},{65,1},{2,66},{66,2},{3,67},{67,3},{4,68},{68... | collective-permute-start | bytes 98312 | tf_op jit(solution)/shard_map/ppermute | solution.py:14
  58.1 5.0 %collective-permute-start.7 = (bf16[64,256]{1,0:T(8,128)(2,1)S(1)}, bf16[64,256]{1,0:T(8,128)(2,1)S(1)}, u32[]{:S(2)}, u32[]{:S(2)}) collective-permute-start(bf16[64,256]{1,0:T(8,128)(2,1)S(1)} %fusion.16), channel_id=1, source_target_pairs={{0,128},{128,0},{1,129},{129,1},{2,130},{130,2},{3,131},{131,3},{4... | collective-permute-start | bytes 98312 | tf_op jit(solution)/shard_map/ppermute | solution.py:14
  63.4 6.4 %collective-permute-start.8 = (bf16[64,256]{1,0:T(8,128)(2,1)S(1)}, bf16[64,256]{1,0:T(8,128)(2,1)S(1)}, u32[]{:S(2)}, u32[]{:S(2)}) collective-permute-start(bf16[64,256]{1,0:T(8,128)(2,1)S(1)} %fusion.17), channel_id=1, source_target_pairs={{0,256},{256,0},{1,257},{257,1},{2,258},{258,2},{3,259},{259,3},{4... | collective-permute-start | bytes 98312 | tf_op jit(solution)/shard_map/ppermute | solution.py:14
  69.9 6.2 %collective-permute-start.9 = (bf16[64,256]{1,0:T(8,128)(2,1)S(1)}, bf16[64,256]{1,0:T(8,128)(2,1)S(1)}, u32[]{:S(2)}, u32[]{:S(2)}) collective-permute-start(bf16[64,256]{1,0:T(8,128)(2,1)S(1)} %fusion.18), channel_id=1, source_target_pairs={{0,256},{256,0},{1,257},{257,1},{2,258},{258,2},{3,259},{259,3},{4... | collective-permute-start | bytes 98312 | tf_op jit(solution)/shard_map/ppermute | solution.py:14
  76.4 4.7 %collective-permute-start.10 = (bf16[64,256]{1,0:T(8,128)(2,1)S(1)}, bf16[64,256]{1,0:T(8,128)(2,1)S(1)}, u32[]{:S(2)}, u32[]{:S(2)}) collective-permute-start(bf16[64,256]{1,0:T(8,128)(2,1)S(1)} %fusion.19), channel_id=1, source_target_pairs={{0,128},{128,0},{1,129},{129,1},{2,130},{130,2},{3,131},{131,3},{4... | collective-permute-start | bytes 98312 | tf_op jit(solution)/shard_map/ppermute | solution.py:14
  81.4 13.4 %collective-permute-start.11 = (bf16[64,256]{1,0:T(8,128)(2,1)S(1)}, bf16[64,256]{1,0:T(8,128)(2,1)S(1)}, u32[]{:S(2)}, u32[]{:S(2)}) collective-permute-start(bf16[64,256]{1,0:T(8,128)(2,1)S(1)} %fusion.20), channel_id=1, source_target_pairs={{0,64},{64,0},{1,65},{65,1},{2,66},{66,2},{3,67},{67,3},{4,68},{68... | collective-permute-start | bytes 98312 | tf_op jit(solution)/shard_map/ppermute | solution.py:14
  95.1 9.3 %collective-permute-start.12 = (bf16[64,256]{1,0:T(8,128)(2,1)S(1)}, bf16[64,256]{1,0:T(8,128)(2,1)S(1)}, u32[]{:S(2)}, u32[]{:S(2)}) collective-permute-start(bf16[64,256]{1,0:T(8,128)(2,1)S(1)} %fusion.21), channel_id=1, source_target_pairs={{0,32},{32,0},{1,33},{33,1},{2,34},{34,2},{3,35},{35,3},{4,36},{36... | collective-permute-start | bytes 98312 | tf_op jit(solution)/shard_map/ppermute | solution.py:14
  104.6 43.1 %copy-start.3 = (bf16[1024,256]{1,0:T(8,128)(2,1)S(1)}, bf16[1024,256]{1,0:T(8,128)(2,1)}, u32[]{:S(2)}) copy-start(bf16[1024,256]{1,0:T(8,128)(2,1)} %param.7) | copy-start | bytes 1572868
  104.8 5.6 %collective-permute-start.13 = (bf16[64,256]{1,0:T(8,128)(2,1)S(1)}, bf16[64,256]{1,0:T(8,128)(2,1)S(1)}, u32[]{:S(2)}, u32[]{:S(2)}) collective-permute-start(bf16[64,256]{1,0:T(8,128)(2,1)S(1)} %fusion.22), channel_id=1, source_target_pairs={{0,16},{16,0},{1,17},{17,1},{2,18},{18,2},{3,19},{19,3},{4,20},{20... | collective-permute-start | bytes 98312 | tf_op jit(solution)/shard_map/ppermute | solution.py:14
  110.7 5.0 %collective-permute-start.14 = (bf16[64,256]{1,0:T(8,128)(2,1)S(1)}, bf16[64,256]{1,0:T(8,128)(2,1)S(1)}, u32[]{:S(2)}, u32[]{:S(2)}) collective-permute-start(bf16[64,256]{1,0:T(8,128)(2,1)S(1)} %fusion.23), channel_id=1, source_target_pairs={{0,8},{8,0},{1,9},{9,1},{2,10},{10,2},{3,11},{11,3},{4,12},{12,4},... | collective-permute-start | bytes 98312 | tf_op jit(solution)/shard_map/ppermute | solution.py:14
  116.0 6.2 %collective-permute-start.15 = (bf16[64,256]{1,0:T(8,128)(2,1)S(1)}, bf16[64,256]{1,0:T(8,128)(2,1)S(1)}, u32[]{:S(2)}, u32[]{:S(2)}) collective-permute-start(bf16[64,256]{1,0:T(8,128)(2,1)S(1)} %fusion.24), channel_id=1, source_target_pairs={{0,4},{4,0},{1,5},{5,1},{2,6},{6,2},{3,7},{7,3},{8,12},{12,8},{9,1... | collective-permute-start | bytes 98312 | tf_op jit(solution)/shard_map/ppermute | solution.py:14
  122.5 4.7 %collective-permute-start.16 = (bf16[64,256]{1,0:T(8,128)(2,1)S(1)}, bf16[64,256]{1,0:T(8,128)(2,1)S(1)}, u32[]{:S(2)}, u32[]{:S(2)}) collective-permute-start(bf16[64,256]{1,0:T(8,128)(2,1)S(1)} %fusion.25), channel_id=1, source_target_pairs={{0,2},{2,0},{1,3},{3,1},{4,6},{6,4},{5,7},{7,5},{8,10},{10,8},{9,1... | collective-permute-start | bytes 98312 | tf_op jit(solution)/shard_map/ppermute | solution.py:14
  127.5 20.0 %collective-permute-start.17 = (bf16[64,256]{1,0:T(8,128)(2,1)S(1)}, bf16[64,256]{1,0:T(8,128)(2,1)S(1)}, u32[]{:S(2)}, u32[]{:S(2)}) collective-permute-start(bf16[64,256]{1,0:T(8,128)(2,1)S(1)} %fusion.26), channel_id=1, source_target_pairs={{0,1},{1,0},{2,3},{3,2},{4,5},{5,4},{6,7},{7,6},{8,9},{9,8},{10,11... | collective-permute-start | bytes 98312 | tf_op jit(solution)/shard_map/ppermute | solution.py:14
where the time goes:
time: 149 us
  starting transfers between devices  78.7 us (53%)
  waiting for transfers between devices  56.9 us (38%)
  matrix products  12.9 us (9%)
    ppermute x18, starting transfers between devices, from_partner(): return lax.ppermute(block, axis, route)  78.7 us
    ppermute x18, waiting for transfers between devices, from_partner(): return lax.ppermute(block, axis, route)  56.9 us
    dot_general x37, matrix products, times_matrix(): return jnp.dot(values, matrix, preferred_element_type=jnp.float32)  9.08 us
    dot_general x19, matrix products, times_transposed(): lax.dot_general(values, matrix, (((1,), (1,)), ((), ())), preferred_eleme...  3.79 us
  transfers between devices with their start and end apart: 18, of which 17 were waited for; matrix products, arithmetic and copies ran while one was open for 4% of the time, Pallas kernels for 0%

commit v1 on v0

v1 whole, which is shorter than its diff:
```python
import jax
import jax.numpy as jnp
from jax import lax
from jax.experimental import pallas as pl
from jax.experimental.pallas import tpu as pltpu
from jax.sharding import PartitionSpec as P


AXIS = "leaf"
BF16 = jnp.bfloat16
F32 = jnp.float32
CHUNKS = 4
VMEM_GRANT = 12 * 2**20


IN_SMEM = pl.BlockSpec(memory_space=pltpu.SMEM)
IN_VMEM = pl.BlockSpec(memory_space=pltpu.VMEM)
IN_HBM = pl.BlockSpec(memory_space=pltpu.HBM)


def swap(block, mask):
    route = [(device, device ^ mask) for device in range(lax.axis_size(AXIS))]
    return lax.ppermute(block, AXIS, route)


def exchange(slots, low, width):
    count, size = lax.axis_size(AXIS), 1 << width
    groups = [
        [base | k << low for k in range(size)]
        for base in range(count)
        if not base & ((size - 1) << low)
    ]
    return lax.all_to_all(slots, AXIS, 0, 0, axis_index_groups=groups)


def times(values, matrix):
    return jnp.dot(values, matrix, preferred_element_type=F32)


def times_t(values, matrix):
    return lax.dot_general(values, matrix, (((1,), (1,)), ((), ())), preferred_element_type=F32)


def product(*matrices):
    total = matrices[0]
    for matrix in matrices[1:]:
        total = times(total, matrix).astype(BF16)
    return total


def call(kernel, outs, ins, specs, scratch=(), grant=VMEM_GRANT):
    outs = [jax.ShapeDtypeStruct(shape, dtype) for shape, dtype in outs]
    return pl.pallas_call(
        kernel,
        out_shape=outs,
        in_specs=specs,
        out_specs=[IN_VMEM] * len(outs),
        scratch_shapes=list(scratch),
        compiler_params=pltpu.CompilerParams(vmem_limit_bytes=grant),
    )(*ins)


def fetched(arrays):
    return [pltpu.VMEM(a.shape, a.dtype) for a in arrays] + [pltpu.SemaphoreType.DMA((len(arrays),))]


def start_copies(pairs, arrived):
    copies = [
        pltpu.make_async_copy(source, target, arrived.at[k])
        for k, (source, target) in enumerate(pairs)
    ]
    for copy in copies:
        copy.start()
    return copies


def chunked(source, held):
    rows = held.shape[0] // CHUNKS
    return [(source.at[pl.ds(k * rows, rows)], held.at[pl.ds(k * rows, rows)]) for k in range(CHUNKS)]


def streamed(sides, held, side_copy, copies):
    rows = held.shape[0] // CHUNKS
    side_copy.wait()
    total = None
    for k in range(CHUNKS):
        copies[k].wait()
        part = times(sides[:, k * rows : (k + 1) * rows], held[k * rows : (k + 1) * rows])
        total = part if total is None else total + part
    return total


def dense_kernel(sides_ref, inverse_ref, out_ref, sides, inverse, sem):
    copies = start_copies([(sides_ref, sides)] + chunked(inverse_ref, inverse), sem)
    out_ref[...] = streamed(sides, inverse, copies[0], copies[1:])


def parts(maps_ref):
    rank = maps_ref.shape[1]
    return [maps_ref[k * rank : (k + 1) * rank] for k in range(maps_ref.shape[0] // rank)]


def open_up_z_kernel(me_ref, part_ref, other_ref, maps_ref, own_ref, slots_ref):
    p, q = parts(maps_ref)[:2]
    own = (part_ref[...] + times(other_ref[...], q)).astype(BF16)
    own_ref[...] = own
    for k in range(4):
        slots_ref[k] = own
    slots_ref[(me_ref[0] >> 3 & 3) ^ 2] = times(own, p).astype(BF16)


def prepare_up_z_kernel(far_ref, own_ref, maps_ref, base_ref, mix_ref, far, sem):
    copies = start_copies([(far_ref, far)], sem)
    p, q = parts(maps_ref)[:2]
    base_ref[...] = times(own_ref[...], product(p, p))
    mix_ref[0] = product(q, p)
    mix_ref[1] = q
    copies[0].wait()
    mix_ref[2] = product(far[...], q)


def close_up_z_kernel(me_ref, got_ref, base_ref, mix_ref, out_ref):
    me = me_ref[0] >> 3 & 3
    total = base_ref[...]
    for k in (1, 2, 3):
        total = total + times(got_ref[me ^ k], mix_ref[k - 1])
    out_ref[...] = total.astype(BF16)


def settle_up_z_kernel(me_ref, got_ref, own_ref, far_ref, maps_ref, out_ref, far, sem):
    copies = start_copies([(far_ref, far)], sem)
    me = me_ref[0] >> 3 & 3
    p, q, c, k = parts(maps_ref)
    own, near = own_ref[...], got_ref[me ^ 1]
    out_ref[0] = (times(near, c) + times(own, k)).astype(BF16)
    middle = (times(own, p) + times(near, q)).astype(BF16)
    copies[0].wait()
    across = (got_ref[me ^ 2].astype(F32) + times(got_ref[me ^ 3], far[...])).astype(BF16)
    out_ref[1] = (times(across, c) + times(middle, k)).astype(BF16)


def open_top_kernel(part_ref, other_ref, maps_ref, own_ref, slots_ref):
    own = (part_ref[...] + times(other_ref[...], parts(maps_ref)[1])).astype(BF16)
    own_ref[...] = own
    for k in range(4):
        slots_ref[k] = own


def eighth_kernel(far_ref, maps_ref, out_ref, far, sem):
    copies = start_copies([(far_ref, far)], sem)
    p, q, c, k = parts(maps_ref)
    copies[0].wait()
    far_p, far_q = parts(far)
    eight, far_eight = {0: p, 1: q}, {2: far_p, 3: far_q}
    nine = {j: product(m, p) for j, m in eight.items()}
    nine |= {j: product(m, q) for j, m in far_eight.items()}
    far_nine = {j: product(m, far_p) for j, m in far_eight.items()}
    far_nine |= {j: product(m, far_q) for j, m in eight.items()}
    for j in range(4):
        total = times_t(nine[j], p) + times_t(far_nine[j], q)
        total = total + (times(eight[j], k) if j in eight else times(far_eight[j], c))
        out_ref[j] = total.astype(BF16)


def prepare_top_kernel(near_ref, eighth_ref, own_ref, maps_ref, base_ref, mix_ref, near, eighth, sem):
    copies = start_copies([(near_ref, near), (eighth_ref, eighth)], sem)
    p, q, c, k = parts(maps_ref)
    for copy in copies:
        copy.wait()
    for j in range(4):
        total = times_t(eighth[j], p) + times_t(near[j ^ 1], q)
        if j < 2:
            total = total + (c if j else k).astype(F32)
        matrix = total.astype(BF16)
        if j:
            mix_ref[j - 1] = matrix
        else:
            base_ref[...] = times(own_ref[...], matrix)


def turn(got_shift, product_of, slot_shift, width):
    def kernel(me_ref, got_ref, base_ref, mix_ref, local_ref, maps_ref, own_ref, slots_ref):
        me = me_ref[0]
        total = base_ref[...]
        for k in (1, 2, 3):
            total = total + product_of(got_ref[(me >> got_shift & 3) ^ k], mix_ref[k - 1])
        node = total.astype(BF16)
        own = times_t(node, parts(maps_ref)[0]) + local_ref[...].astype(F32)
        own = own.astype(BF16)
        own_ref[...] = own
        place, half = me >> slot_shift & (1 << width) - 1, 1 << width - 1
        near = place & half
        for k in range(half):
            slots_ref[near | k] = own
            slots_ref[(near ^ half) | k] = node

    return kernel


def prepare_down_kernel(far_ref, own_ref, local_ref, maps_ref, base_ref, mix_ref, far, sem):
    copies = start_copies([(far_ref, far)], sem)
    p, q = parts(maps_ref)[:2]
    base_ref[...] = times_t(own_ref[...], p) + local_ref[...].astype(F32)
    mix_ref[0] = q
    mix_ref[1] = product(p, q)
    copies[0].wait()
    mix_ref[2] = product(q, far[...])


def prepare_down_y_kernel(*refs):
    (core_ref, y1_ref, cy_ref, dense_ref, own_ref, one_ref, two_ref, maps_ref, basis_ref) = refs[:9]
    base_ref, mix_ref, core, y1, cy, dense, sem = refs[9:]
    copies = start_copies([(core_ref, core), (y1_ref, y1), (cy_ref, cy), (dense_ref, dense)], sem)
    p, q = parts(maps_ref)[:2]
    mix = [product(p, p), None, product(p, q), None]
    for copy in copies:
        copy.wait()
    rank = p.shape[0]
    core_p, core_q, core_two = core[:rank], core[rank : 2 * rank], core[2 * rank :]
    mix[1] = product(q, core_p)
    mix[3] = product(q, core_q)
    node = times_t(own_ref[...], mix[0]) + one_ref[...].astype(F32)
    node = node + times_t(two_ref[...], p) + times_t(core_two, q)
    base_ref[...] = dense[...] + times_t(node.astype(BF16), basis_ref[...])
    for k, far in enumerate((q, core_q, y1[...], cy[...])):
        if k:
            mix_ref[k - 1] = mix[k]
        mix_ref[k + 3] = product(mix[k], far)


def finish_kernel(me_ref, got_ref, base_ref, mix_ref, basis_ref, out_ref):
    me = me_ref[0] & 7
    total = None
    for k in range(1, 8):
        part = times_t(got_ref[me ^ k], mix_ref[k - 1])
        total = part if total is None else total + part
    node = total.astype(BF16)
    out_ref[...] = (base_ref[...] + times_t(node, basis_ref[...])).astype(BF16)


def body(right_sides, leaf_inverse, leaf_basis, transfer, coupling):
    rank = leaf_basis.shape[1]
    columns = right_sides.shape[0]
    block, square = (columns, rank), (rank, rank)
    me = lax.axis_index(AXIS).astype(jnp.int32).reshape(1)
    prefetched, local = {}, {}

    def after(values, late):
        return lax.optimization_barrier((values, late))[0]

    def prefetch(name, value, mask, late):
        value = after(value, late)
        prefetched[name] = swap(value, mask)

    current = times(right_sides, leaf_basis).astype(BF16)
    own_map, other_map = transfer[:rank], transfer[rank:]
    from_other, from_own = coupling[:rank], coupling[rank:]

    def settle(level, far, own, late):
        far, own = after((far, own), late)
        total = times(far, from_other) + times(own, from_own)
        local[level] = lax.optimization_barrier(total.astype(BF16))

    def half_up(current, bit):
        other = swap(current, 1 << bit)
        part = times(current, own_map)
        return part, other

    def up(current, bit):
        part, other = half_up(current, bit)
        above = (part + times(other, other_map)).astype(BF16)
        settle(bit + 1, other, current, above)
        return above

    current = up(current, 0)
    maps = jnp.concatenate(after((transfer, coupling), current), 0)
    prefetch("pre_q_z2", after(transfer, current)[rank:], 16, current)
    current = up(current, 1)
    prefetch("pre_x2", transfer, 256, current)
    below = current
    part, other = half_up(below, 2)

    current, slots = call(
        open_up_z_kernel,
        [(block, BF16), ((4, *block), BF16)],
        [me, part, other, maps],
        [IN_SMEM] + [IN_VMEM] * 3,
    )
    settle(3, other, below, current)
    far = prefetched["pre_x2"]
    (eighth,) = call(
        eighth_kernel,
        [((4, *square), BF16)],
        [far, after(maps, slots)],
        [IN_HBM, IN_VMEM],
        fetched([far]),
    )
    prefetch("pre_x1", eighth, 128, slots)
    got = exchange(slots, 3, 2)
    far = prefetched["pre_q_z2"]
    base, mix = call(
        prepare_up_z_kernel,
        [(block, F32), ((3, *square), BF16)],
        [far, current, maps],
        [IN_HBM] + [IN_VMEM] * 2,
        fetched([far]),
    )
    below = current
    (current,) = call(
        close_up_z_kernel, [(block, BF16)], [me, got, base, mix], [IN_SMEM] + [IN_VMEM] * 3
    )
    (settled,) = call(
        settle_up_z_kernel,
        [((2, *block), BF16)],
        [me, got, after(below, current), far, maps],
        [IN_SMEM, IN_VMEM, IN_VMEM, IN_HBM, IN_VMEM],
        fetched([far]),
    )
    current = up(current, 5)
    below = current
    part, other = half_up(below, 6)

    current, slots = call(
        open_top_kernel, [(block, BF16), ((4, *block), BF16)], [part, other, maps], [IN_VMEM] * 3
    )
    settle(7, other, below, current)
    prefetch("pre_q_z4", after(transfer, slots)[rank:], 32, slots)
    got = exchange(slots, 7, 2)
    near = prefetched["pre_x1"]
    base, mix = call(
        prepare_top_kernel,
        [(block, F32), ((3, *square), BF16)],
        [near, eighth, current, maps],
        [IN_HBM] * 2 + [IN_VMEM] * 2,
        fetched([near, eighth]),
    )
    local[4], local[5] = settled[0], settled[1]

    def turn_down(kernel, got, base, mix, level, width):
        return call(
            kernel,
            [(block, BF16), ((1 << width, *block), BF16)],
            [me, got, base, mix, local[level], maps],
            [IN_SMEM] + [IN_VMEM] * 5,
        )

    def prepare_down(far, own, level):
        return call(
            prepare_down_kernel,
            [(block, F32), ((3, *square), BF16)],
            [far, own, local[level], maps],
            [IN_HBM] + [IN_VMEM] * 3,
            fetched([far]),
        )

    own, slots = turn_down(turn(7, times, 5, 2), got, base, mix, 7, 2)
    neighbour_map = after(transfer, slots)[rank:]
    prefetch("pre_q_y1", neighbour_map, 2, slots)
    prefetch("pre_q_cy", neighbour_map, 3, slots)
    prefetch("pre_q_z1", neighbour_map, 8, slots)
    got = exchange(slots, 5, 2)
    base, mix = prepare_down(prefetched["pre_q_z4"], own, 6)

    own, slots = turn_down(turn(5, times_t, 3, 2), got, base, mix, 5, 2)
    prefetch("pre_core", jnp.concatenate(after((maps[: 2 * rank], local[2]), slots), 0), 1, slots)
    got = exchange(slots, 3, 2)
    base, mix = prepare_down(prefetched["pre_q_z1"], own, 4)

    own, slots = turn_down(turn(3, times_t, 0, 3), got, base, mix, 3, 3)
    got = exchange(slots, 0, 3)
    copied = [right_sides, leaf_inverse]
    (dense,) = call(
        dense_kernel,
        [((columns, leaf_inverse.shape[1]), F32)],
        [after(right_sides, slots), leaf_inverse],
        [IN_HBM] * 2,
        [pltpu.VMEM(a.shape, a.dtype) for a in copied] + [pltpu.SemaphoreType.DMA((CHUNKS + 1,))],
        None,
    )
    near = [prefetched[f"pre_{name}"] for name in ("core", "q_y1", "q_cy")]
    base, mix = call(
        prepare_down_y_kernel,
        [(dense.shape, F32), ((7, *square), BF16)],
        [*near, dense, own, local[1], local[2], maps, leaf_basis],
        [IN_HBM] * 4 + [IN_VMEM] * 5,
        fetched([*near, dense]),
    )
    (out,) = call(
        finish_kernel,
        [(dense.shape, BF16)],
        [me, got, base, mix, leaf_basis],
        [IN_SMEM] + [IN_VMEM] * 4,
    )
    return out


def solution(mesh):
    placed = (P(None, AXIS), P(AXIS, None), P(AXIS, None), P(AXIS, None), P(AXIS, None))
    return jax.shard_map(
        body, mesh=mesh, in_specs=placed, out_specs=P(None, AXIS), check_vma=False
    )
```

time: 149 us -> 140 us (0.940)
  waiting for transfers between devices: 56.9 us -> 22.3 us
  Pallas kernels: 0 us -> 15.3 us
  starting transfers between devices: 78.7 us -> 90.2 us
  matrix products: 12.9 us -> 7.58 us
  local copies, waits for them, and re-layouts: 0.06 us -> 2.93 us
    ppermute x18 -> x13, waiting for transfers between devices: 56.9 us -> 17.4 us  [swap(): return lax.ppermute(block, AXIS, route)]
    all_to_all x0 -> x5, starting transfers between devices: none -> 26.1 us  [exchange(): return lax.all_to_all(slots, AXIS, 0, 0, axis_index_groups=groups)]
    pallas_call x0 -> x15, Pallas kernels: none -> 15.3 us  [call(): pl.pallas_call(kernel, out_shape=outs, in_specs=specs, out_specs=[IN_VMEM...]
    ppermute x18 -> x13, starting transfers between devices: 78.7 us -> 64.2 us  [swap(): return lax.ppermute(block, AXIS, route)]
    dot_general x56 -> x19, matrix products: 12.9 us -> 7.58 us  [times(): return jnp.dot(values, matrix, preferred_element_type=F32)]
    all_to_all x0 -> x5, waiting for transfers between devices: none -> 4.88 us  [exchange(): return lax.all_to_all(slots, AXIS, 0, 0, axis_index_groups=groups)]
    unnamed x8 -> x9, local copies, waits for them, and re-layouts: 0.06 us -> 1.93 us
  transfers between devices with their start and end apart: 18 -> 18, of which waited for: 17 -> 6; matrix products, arithmetic and copies ran while one was open for 4% -> 5% of each run, Pallas kernels for 0% -> 8%
where the time goes in v1:
time: 140 us; the launch traced here: 139 us
  starting transfers between devices  90.2 us (64%)
  waiting for transfers between devices  22.3 us (16%)
  Pallas kernels  15.3 us (11%)
  matrix products  7.58 us (5%)
  local copies, waits for them, and re-layouts  2.93 us (2%)
    ppermute x13, starting transfers between devices, swap(): return lax.ppermute(block, AXIS, route)  64.2 us
    all_to_all x5, starting transfers between devices, exchange(): return lax.all_to_all(slots, AXIS, 0, 0, axis_index_groups=groups)  26.1 us
    ppermute x13, waiting for transfers between devices, swap(): return lax.ppermute(block, AXIS, route)  17.4 us
    pallas_call x15, Pallas kernels, call(): pl.pallas_call(kernel, out_shape=outs, in_specs=specs, out_specs=[IN_VMEM...  15.3 us
    dot_general x19, matrix products, times(): return jnp.dot(values, matrix, preferred_element_type=F32)  7.58 us
    all_to_all x5, waiting for transfers between devices, exchange(): return lax.all_to_all(slots, AXIS, 0, 0, axis_index_groups=groups)  4.88 us
  transfers between devices with their start and end apart: 18, of which 6 were waited for; matrix products, arithmetic and copies ran while one was open for 5% of the time, Pallas kernels for 8%

profile of v1, /device:TPU:1, one launch (start us, length us, event | category | flops | bytes accessed | tf_op | source)
XLA Modules:
  0.0 138.7 jit_solution(13708689386104298510)
XLA Ops:
  0.0 1.4 convolution_convert_fusion
  1.4 8.7 %collective-permute-start = (bf16[64,256]{1,0:T(8,128)(2,1)S(1)}, bf16[64,256]{1,0:T(8,128)(2,1)S(1)}, u32[]{:S(2)}, u32[]{:S(2)}) collective-permute-start(bf16[64,256]{1,0:T(8,128)(2,1)S(1)} %convolution_convert_fusion), channel_id=1, source_target_pairs={{0,1},{1,0},{2,3},{3,2},{4,5},{5,4},{6,7},{7,6},{8,9},{9,8},{10,11... | collective-permute-start | bytes 98312 | tf_op jit(solution)/shard_map/ppermute | solution.py:23
  10.1 1.0 fusion.34
  11.2 1.1 fusion
  12.2 1.9 %collective-permute-start.1 = (bf16[64,256]{1,0:T(8,128)(2,1)S(1)}, bf16[64,256]{1,0:T(8,128)(2,1)S(1)}, u32[]{:S(2)}, u32[]{:S(2)}) collective-permute-start(bf16[64,256]{1,0:T(8,128)(2,1)S(1)} %fusion), channel_id=1, source_target_pairs={{0,2},{1,3},{2,0},{3,1},{4,6},{5,7},{6,4},{7,5},{8,10},{9,11},{10,... | collective-permute-start | bytes 98312 | tf_op jit(solution)/shard_map/ppermute | solution.py:23
  14.2 1.0 fusion.32
  15.2 1.1 fusion.12
  17.2 1.9 %collective-permute-start.3 = (bf16[256,256]{1,0:T(8,128)(2,1)S(1)}, bf16[256,256]{1,0:T(8,128)(2,1)S(1)}, u32[]{:S(2)}, u32[]{:S(2)}) collective-permute-start(bf16[256,256]{1,0:T(8,128)(2,1)S(1)} %slice.29), channel_id=1, source_target_pairs={{0,16},{1,17},{2,18},{3,19},{4,20},{5,21},{6,22},{7,23},{8,24},{9,... | collective-permute-start | bytes 393224 | tf_op jit(solution)/shard_map/ppermute | solution.py:23
  20.3 3.5 %collective-permute-start.2 = (bf16[64,256]{1,0:T(8,128)(2,1)S(1)}, bf16[64,256]{1,0:T(8,128)(2,1)S(1)}, u32[]{:S(2)}, u32[]{:S(2)}) collective-permute-start(bf16[64,256]{1,0:T(8,128)(2,1)S(1)} %fusion.1), channel_id=1, source_target_pairs={{0,4},{1,5},{2,6},{3,7},{4,0},{5,1},{6,2},{7,3},{8,12},{9,13},{10,... | collective-permute-start | bytes 98312 | tf_op jit(solution)/shard_map/ppermute | solution.py:23
  23.9 4.7 %collective-permute-start.6 = (bf16[512,256]{1,0:T(8,128)(2,1)S(1)}, bf16[512,256]{1,0:T(8,128)(2,1)S(1)}, u32[]{:S(2)}, u32[]{:S(2)}) collective-permute-start(bf16[512,256]{1,0:T(8,128)(2,1)S(1)} %copy-done.2), channel_id=1, source_target_pairs={{0,256},{1,257},{2,258},{3,259},{4,260},{5,261},{6,262},{7,263},{8... | collective-permute-start | bytes 786440 | tf_op jit(solution)/shard_map/ppermute | solution.py:23
  29.5 3.3 %all-to-all-start = ((bf16[4,64,256]{2,1,0:T(8,128)(2,1)}), bf16[4,64,256]{2,1,0:T(8,128)(2,1)S(1)}, u32[]{:S(2)}, u32[]{:S(2)}) async-start(bf16[4,64,256]{2,1,0:T(8,128)(2,1)} %get-tuple-element.53), calls=%async_computation | async-start | bytes 262144 | tf_op jit(solution)/shard_map/all_to_all | solution.py:33
  35.2 3.1 %collective-permute-start.7 = (bf16[4,256,256]{2,1,0:T(8,128)(2,1)S(1)}, bf16[4,256,256]{2,1,0:T(8,128)(2,1)S(1)}, u32[]{:S(2)}, u32[]{:S(2)}) collective-permute-start(bf16[4,256,256]{2,1,0:T(8,128)(2,1)S(1)} %shard_map.59.eighth_ref), channel_id=1, source_target_pairs={{0,128},{1,129},{2,130},{3,131},{4,132},{5,133},{6,134},{7,135},{8... | collective-permute-start | bytes 1572872 | tf_op jit(solution)/shard_map/ppermute | solution.py:23
  38.5 8.8 %collective-permute-start.4 = (bf16[64,256]{1,0:T(8,128)(2,1)S(1)}, bf16[64,256]{1,0:T(8,128)(2,1)S(1)}, u32[]{:S(2)}, u32[]{:S(2)}) collective-permute-start(bf16[64,256]{1,0:T(8,128)(2,1)S(1)} %shard_map.57), channel_id=1, source_target_pairs={{0,32},{1,33},{2,34},{3,35},{4,36},{5,37},{6,38},{7,39},{8,40},{9,... | collective-permute-start | bytes 98312 | tf_op jit(solution)/shard_map/ppermute | solution.py:23
  49.0 12.1 %collective-permute-start.5 = (bf16[64,256]{1,0:T(8,128)(2,1)S(1)}, bf16[64,256]{1,0:T(8,128)(2,1)S(1)}, u32[]{:S(2)}, u32[]{:S(2)}) collective-permute-start(bf16[64,256]{1,0:T(8,128)(2,1)S(1)} %fusion.2), channel_id=1, source_target_pairs={{0,64},{1,65},{2,66},{3,67},{4,68},{5,69},{6,70},{7,71},{8,72},{9,... | collective-permute-start | bytes 98312 | tf_op jit(solution)/shard_map/ppermute | solution.py:23
  61.2 1.2 collective-permute-done.5.other_ref
  63.2 4.1 %all-to-all-start.1 = ((bf16[4,64,256]{2,1,0:T(8,128)(2,1)}), bf16[4,64,256]{2,1,0:T(8,128)(2,1)S(1)}, u32[]{:S(2)}, u32[]{:S(2)}) async-start(bf16[4,64,256]{2,1,0:T(8,128)(2,1)} %get-tuple-element.59), calls=%async_computation.1 | async-start | bytes 262144 | tf_op jit(solution)/shard_map/all_to_all | solution.py:33
  68.5 3.6 %all-to-all-done.1.got_ref = bf16[4,64,256]{2,1,0:T(8,128)(2,1)S(1)} async-done(((bf16[4,64,256]{2,1,0:T(8,128)(2,1)}), bf16[4,64,256]{2,1,0:T(8,128)(2,1)S(1)}, u32[]{:S(2)}, u32[]{:S(2)}) %all-to-all-start.1) | async-done | bytes 131104 | tf_op jit(solution)/shard_map/all_to_all | solution.py:33
  73.2 11.2 %all-to-all-start.2 = ((bf16[4,64,256]{2,1,0:T(8,128)(2,1)}), bf16[4,64,256]{2,1,0:T(8,128)(2,1)S(1)}, u32[]{:S(2)}, u32[]{:S(2)}) async-start(bf16[4,64,256]{2,1,0:T(8,128)(2,1)} %get-tuple-element.68), calls=%async_computation.2 | async-start | bytes 262144 | tf_op jit(solution)/shard_map/all_to_all | solution.py:33
  84.5 7.3 %collective-permute-start.8 = (bf16[256,256]{1,0:T(8,128)(2,1)S(1)}, bf16[256,256]{1,0:T(8,128)(2,1)S(1)}, u32[]{:S(2)}, u32[]{:S(2)}) collective-permute-start(bf16[256,256]{1,0:T(8,128)(2,1)S(1)} %slice.32), channel_id=1, source_target_pairs={{0,32},{1,33},{2,34},{3,35},{4,36},{5,37},{6,38},{7,39},{8,40},{9,... | collective-permute-start | bytes 393224 | tf_op jit(solution)/shard_map/ppermute | solution.py:23
  91.9 15.4 %collective-permute-done.8.far_ref = bf16[256,256]{1,0:T(8,128)(2,1)S(1)} collective-permute-done((bf16[256,256]{1,0:T(8,128)(2,1)S(1)}, bf16[256,256]{1,0:T(8,128)(2,1)S(1)}, u32[]{:S(2)}, u32[]{:S(2)}) %collective-permute-start.8) | collective-permute-done | bytes 131104 | tf_op jit(solution)/shard_map/ppermute | solution.py:23
  108.0 1.1 shard_map.64
  109.0 3.3 %all-to-all-start.3 = ((bf16[4,64,256]{2,1,0:T(8,128)(2,1)}), bf16[4,64,256]{2,1,0:T(8,128)(2,1)S(1)}, u32[]{:S(2)}, u32[]{:S(2)}) async-start(bf16[4,64,256]{2,1,0:T(8,128)(2,1)} %get-tuple-element.77), calls=%async_computation.3 | async-start | bytes 262144 | tf_op jit(solution)/shard_map/all_to_all | solution.py:33
  112.5 3.3 %collective-permute-start.9 = (bf16[256,256]{1,0:T(8,128)(2,1)S(1)}, bf16[256,256]{1,0:T(8,128)(2,1)S(1)}, u32[]{:S(2)}, u32[]{:S(2)}) collective-permute-start(bf16[256,256]{1,0:T(8,128)(2,1)S(1)} %slice.34), channel_id=1, source_target_pairs={{0,8},{1,9},{2,10},{3,11},{4,12},{5,13},{6,14},{7,15},{8,0},{9,1},... | collective-permute-start | bytes 393224 | tf_op jit(solution)/shard_map/ppermute | solution.py:23
  115.9 3.6 %collective-permute-start.10 = (bf16[576,256]{1,0:T(8,128)(2,1)S(1)}, bf16[576,256]{1,0:T(8,128)(2,1)S(1)}, u32[]{:S(2)}, u32[]{:S(2)}) collective-permute-start(bf16[576,256]{1,0:T(8,128)(2,1)S(1)} %pad_maximum_fusion), channel_id=1, source_target_pairs={{0,1},{1,0},{2,3},{3,2},{4,5},{5,4},{6,7},{7,6},{8,9},{9,8},{10,11... | collective-permute-start | bytes 884744 | tf_op jit(solution)/shard_map/ppermute | solution.py:23
  119.7 1.9 %collective-permute-start.12 = (bf16[256,256]{1,0:T(8,128)(2,1)S(1)}, bf16[256,256]{1,0:T(8,128)(2,1)S(1)}, u32[]{:S(2)}, u32[]{:S(2)}) collective-permute-start(bf16[256,256]{1,0:T(8,128)(2,1)S(1)} %slice.34), channel_id=1, source_target_pairs={{0,3},{1,2},{2,1},{3,0},{4,7},{5,6},{6,5},{7,4},{8,11},{9,10},{10,... | collective-permute-start | bytes 393224 | tf_op jit(solution)/shard_map/ppermute | solution.py:23
  121.6 3.3 %collective-permute-start.11 = (bf16[256,256]{1,0:T(8,128)(2,1)S(1)}, bf16[256,256]{1,0:T(8,128)(2,1)S(1)}, u32[]{:S(2)}, u32[]{:S(2)}) collective-permute-start(bf16[256,256]{1,0:T(8,128)(2,1)S(1)} %slice.34), channel_id=1, source_target_pairs={{0,2},{1,3},{2,0},{3,1},{4,6},{5,7},{6,4},{7,5},{8,10},{9,11},{10,... | collective-permute-start | bytes 393224 | tf_op jit(solution)/shard_map/ppermute | solution.py:23
  125.5 1.1 shard_map.66
  126.6 4.1 %all-to-all-start.4 = ((bf16[8,64,256]{2,1,0:T(8,128)(2,1)}), bf16[8,64,256]{2,1,0:T(8,128)(2,1)S(1)}, u32[]{:S(2)}, u32[]{:S(2)}) async-start(bf16[8,64,256]{2,1,0:T(8,128)(2,1)} %get-tuple-element.85), calls=%async_computation.4 | async-start | bytes 524288 | tf_op jit(solution)/shard_map/all_to_all | solution.py:33
  130.8 2.6 %shard_map.67.refs_3_ = f32[64,1024]{1,0:T(8,128)} custom-call(bf16[64,1024]{1,0:T(8,128)(2,1)} %sides_ref, bf16[1024,1024]{1,0:T(8,128)(2,1)} %inverse_ref.1), custom_call_target="tpu_custom_call" | custom-call | tf_op jit(solution)/shard_map/pallas_call | solution.py:53
  134.4 1.5 %shard_map.68 = (f32[64,1024]{1,0:T(8,128)S(1)}, bf16[7,256,256]{2,1,0:T(8,128)(2,1)S(1)}) custom-call(bf16[576,256]{1,0:T(8,128)(2,1)S(1)} %collective-permute-done.10.refs_0_, bf16[256,256]{1,0:T(8,128)(2,1)S(1)} %collective-permute-done.11.refs_1_, bf16[256,256]{1,0:T(8,128)(2,1)S(1)} %collective-permute-done.12.refs_2_, f32[64,1024]{1,0:T(8,128)S(1)} %copy-done.1, ...), custom_call_target="tpu_custom_call" | custom-call | tf_op jit(solution)/shard_map/pallas_call | solution.py:53
  135.9 1.3 all-to-all-done.4.got_ref
  137.2 1.5 %shard_map.69 = bf16[64,1024]{1,0:T(8,128)(2,1)} custom-call(s32[1]{0:T(128)} %bitcast.me_ref, bf16[8,64,256]{2,1,0:T(8,128)(2,1)S(1)} %all-to-all-done.4.got_ref, f32[64,1024]{1,0:T(8,128)S(1)} %get-tuple-element.95.base_ref, bf16[7,256,256]{2,1,0:T(8,128)(2,1)S(1)} %get-tuple-element.96.mix_ref, bf16[1024,256]{1,0:T(8,128)(2,1)S(1)} %copy-done), custom_call_target="tpu_custom_call" | custom-call | tf_op jit(solution)/shard_map/pallas_call | solution.py:53
  (53 shorter events, 13.3 us)
Async XLA Ops:
  0.0 20.2 %copy-start.2 = (bf16[512,256]{1,0:T(8,128)(2,1)S(1)}, bf16[512,256]{1,0:T(8,128)(2,1)}, u32[]{:S(2)}) copy-start(bf16[512,256]{1,0:T(8,128)(2,1)} %param.8) | copy-start | bytes 786436
  0.0 20.1 %copy-start.3 = (bf16[512,256]{1,0:T(8,128)(2,1)S(1)}, bf16[512,256]{1,0:T(8,128)(2,1)}, u32[]{:S(2)}) copy-start(bf16[512,256]{1,0:T(8,128)(2,1)} %param.9) | copy-start | bytes 786436
  1.4 9.8 %collective-permute-start = (bf16[64,256]{1,0:T(8,128)(2,1)S(1)}, bf16[64,256]{1,0:T(8,128)(2,1)S(1)}, u32[]{:S(2)}, u32[]{:S(2)}) collective-permute-start(bf16[64,256]{1,0:T(8,128)(2,1)S(1)} %convolution_convert_fusion), channel_id=1, source_target_pairs={{0,1},{1,0},{2,3},{3,2},{4,5},{5,4},{6,7},{7,6},{8,9},{9,8},{10,11... | collective-permute-start | bytes 98312 | tf_op jit(solution)/shard_map/ppermute | solution.py:23
  12.2 7.9 %collective-permute-start.1 = (bf16[64,256]{1,0:T(8,128)(2,1)S(1)}, bf16[64,256]{1,0:T(8,128)(2,1)S(1)}, u32[]{:S(2)}, u32[]{:S(2)}) collective-permute-start(bf16[64,256]{1,0:T(8,128)(2,1)S(1)} %fusion), channel_id=1, source_target_pairs={{0,2},{1,3},{2,0},{3,1},{4,6},{5,7},{6,4},{7,5},{8,10},{9,11},{10,... | collective-permute-start | bytes 98312 | tf_op jit(solution)/shard_map/ppermute | solution.py:23
  17.2 16.0 %collective-permute-start.3 = (bf16[256,256]{1,0:T(8,128)(2,1)S(1)}, bf16[256,256]{1,0:T(8,128)(2,1)S(1)}, u32[]{:S(2)}, u32[]{:S(2)}) collective-permute-start(bf16[256,256]{1,0:T(8,128)(2,1)S(1)} %slice.29), channel_id=1, source_target_pairs={{0,16},{1,17},{2,18},{3,19},{4,20},{5,21},{6,22},{7,23},{8,24},{9,... | collective-permute-start | bytes 393224 | tf_op jit(solution)/shard_map/ppermute | solution.py:23
  20.3 8.3 %collective-permute-start.2 = (bf16[64,256]{1,0:T(8,128)(2,1)S(1)}, bf16[64,256]{1,0:T(8,128)(2,1)S(1)}, u32[]{:S(2)}, u32[]{:S(2)}) collective-permute-start(bf16[64,256]{1,0:T(8,128)(2,1)S(1)} %fusion.1), channel_id=1, source_target_pairs={{0,4},{1,5},{2,6},{3,7},{4,0},{5,1},{6,2},{7,3},{8,12},{9,13},{10,... | collective-permute-start | bytes 98312 | tf_op jit(solution)/shard_map/ppermute | solution.py:23
  23.9 10.3 %collective-permute-start.6 = (bf16[512,256]{1,0:T(8,128)(2,1)S(1)}, bf16[512,256]{1,0:T(8,128)(2,1)S(1)}, u32[]{:S(2)}, u32[]{:S(2)}) collective-permute-start(bf16[512,256]{1,0:T(8,128)(2,1)S(1)} %copy-done.2), channel_id=1, source_target_pairs={{0,256},{1,257},{2,258},{3,259},{4,260},{5,261},{6,262},{7,263},{8... | collective-permute-start | bytes 786440 | tf_op jit(solution)/shard_map/ppermute | solution.py:23
  29.5 8.8 %all-to-all-start = ((bf16[4,64,256]{2,1,0:T(8,128)(2,1)}), bf16[4,64,256]{2,1,0:T(8,128)(2,1)S(1)}, u32[]{:S(2)}, u32[]{:S(2)}) async-start(bf16[4,64,256]{2,1,0:T(8,128)(2,1)} %get-tuple-element.53), calls=%async_computation | async-start | bytes 262144 | tf_op jit(solution)/shard_map/all_to_all | solution.py:33
  35.2 32.4 %collective-permute-start.7 = (bf16[4,256,256]{2,1,0:T(8,128)(2,1)S(1)}, bf16[4,256,256]{2,1,0:T(8,128)(2,1)S(1)}, u32[]{:S(2)}, u32[]{:S(2)}) collective-permute-start(bf16[4,256,256]{2,1,0:T(8,128)(2,1)S(1)} %shard_map.59.eighth_ref), channel_id=1, source_target_pairs={{0,128},{1,129},{2,130},{3,131},{4,132},{5,133},{6,134},{7,135},{8... | collective-permute-start | bytes 1572872 | tf_op jit(solution)/shard_map/ppermute | solution.py:23
  38.5 10.1 %collective-permute-start.4 = (bf16[64,256]{1,0:T(8,128)(2,1)S(1)}, bf16[64,256]{1,0:T(8,128)(2,1)S(1)}, u32[]{:S(2)}, u32[]{:S(2)}) collective-permute-start(bf16[64,256]{1,0:T(8,128)(2,1)S(1)} %shard_map.57), channel_id=1, source_target_pairs={{0,32},{1,33},{2,34},{3,35},{4,36},{5,37},{6,38},{7,39},{8,40},{9,... | collective-permute-start | bytes 98312 | tf_op jit(solution)/shard_map/ppermute | solution.py:23
  49.0 13.4 %collective-permute-start.5 = (bf16[64,256]{1,0:T(8,128)(2,1)S(1)}, bf16[64,256]{1,0:T(8,128)(2,1)S(1)}, u32[]{:S(2)}, u32[]{:S(2)}) collective-permute-start(bf16[64,256]{1,0:T(8,128)(2,1)S(1)} %fusion.2), channel_id=1, source_target_pairs={{0,64},{1,65},{2,66},{3,67},{4,68},{5,69},{6,70},{7,71},{8,72},{9,... | collective-permute-start | bytes 98312 | tf_op jit(solution)/shard_map/ppermute | solution.py:23
  63.2 9.0 %all-to-all-start.1 = ((bf16[4,64,256]{2,1,0:T(8,128)(2,1)}), bf16[4,64,256]{2,1,0:T(8,128)(2,1)S(1)}, u32[]{:S(2)}, u32[]{:S(2)}) async-start(bf16[4,64,256]{2,1,0:T(8,128)(2,1)} %get-tuple-element.59), calls=%async_computation.1 | async-start | bytes 262144 | tf_op jit(solution)/shard_map/all_to_all | solution.py:33
  73.2 34.8 %all-to-all-start.2 = ((bf16[4,64,256]{2,1,0:T(8,128)(2,1)}), bf16[4,64,256]{2,1,0:T(8,128)(2,1)S(1)}, u32[]{:S(2)}, u32[]{:S(2)}) async-start(bf16[4,64,256]{2,1,0:T(8,128)(2,1)} %get-tuple-element.68), calls=%async_computation.2 | async-start | bytes 262144 | tf_op jit(solution)/shard_map/all_to_all | solution.py:33
  84.5 22.9 %collective-permute-start.8 = (bf16[256,256]{1,0:T(8,128)(2,1)S(1)}, bf16[256,256]{1,0:T(8,128)(2,1)S(1)}, u32[]{:S(2)}, u32[]{:S(2)}) collective-permute-start(bf16[256,256]{1,0:T(8,128)(2,1)S(1)} %slice.32), channel_id=1, source_target_pairs={{0,32},{1,33},{2,34},{3,35},{4,36},{5,37},{6,38},{7,39},{8,40},{9,... | collective-permute-start | bytes 393224 | tf_op jit(solution)/shard_map/ppermute | solution.py:23
  109.0 16.5 %all-to-all-start.3 = ((bf16[4,64,256]{2,1,0:T(8,128)(2,1)}), bf16[4,64,256]{2,1,0:T(8,128)(2,1)S(1)}, u32[]{:S(2)}, u32[]{:S(2)}) async-start(bf16[4,64,256]{2,1,0:T(8,128)(2,1)} %get-tuple-element.77), calls=%async_computation.3 | async-start | bytes 262144 | tf_op jit(solution)/shard_map/all_to_all | solution.py:33
  112.5 12.3 %collective-permute-start.9 = (bf16[256,256]{1,0:T(8,128)(2,1)S(1)}, bf16[256,256]{1,0:T(8,128)(2,1)S(1)}, u32[]{:S(2)}, u32[]{:S(2)}) collective-permute-start(bf16[256,256]{1,0:T(8,128)(2,1)S(1)} %slice.34), channel_id=1, source_target_pairs={{0,8},{1,9},{2,10},{3,11},{4,12},{5,13},{6,14},{7,15},{8,0},{9,1},... | collective-permute-start | bytes 393224 | tf_op jit(solution)/shard_map/ppermute | solution.py:23
  115.9 17.5 %collective-permute-start.10 = (bf16[576,256]{1,0:T(8,128)(2,1)S(1)}, bf16[576,256]{1,0:T(8,128)(2,1)S(1)}, u32[]{:S(2)}, u32[]{:S(2)}) collective-permute-start(bf16[576,256]{1,0:T(8,128)(2,1)S(1)} %pad_maximum_fusion), channel_id=1, source_target_pairs={{0,1},{1,0},{2,3},{3,2},{4,5},{5,4},{6,7},{7,6},{8,9},{9,8},{10,11... | collective-permute-start | bytes 884744 | tf_op jit(solution)/shard_map/ppermute | solution.py:23
  119.7 13.7 %collective-permute-start.12 = (bf16[256,256]{1,0:T(8,128)(2,1)S(1)}, bf16[256,256]{1,0:T(8,128)(2,1)S(1)}, u32[]{:S(2)}, u32[]{:S(2)}) collective-permute-start(bf16[256,256]{1,0:T(8,128)(2,1)S(1)} %slice.34), channel_id=1, source_target_pairs={{0,3},{1,2},{2,1},{3,0},{4,7},{5,6},{6,5},{7,4},{8,11},{9,10},{10,... | collective-permute-start | bytes 393224 | tf_op jit(solution)/shard_map/ppermute | solution.py:23
  121.6 11.8 %collective-permute-start.11 = (bf16[256,256]{1,0:T(8,128)(2,1)S(1)}, bf16[256,256]{1,0:T(8,128)(2,1)S(1)}, u32[]{:S(2)}, u32[]{:S(2)}) collective-permute-start(bf16[256,256]{1,0:T(8,128)(2,1)S(1)} %slice.34), channel_id=1, source_target_pairs={{0,2},{1,3},{2,0},{3,1},{4,6},{5,7},{6,4},{7,5},{8,10},{9,11},{10,... | collective-permute-start | bytes 393224 | tf_op jit(solution)/shard_map/ppermute | solution.py:23
  125.5 7.9 %copy-start = (bf16[1024,256]{1,0:T(8,128)(2,1)S(1)}, bf16[1024,256]{1,0:T(8,128)(2,1)}, u32[]{:S(2)}) copy-start(bf16[1024,256]{1,0:T(8,128)(2,1)} %basis_ref.1) | copy-start | bytes 1572868
  126.6 10.6 %all-to-all-start.4 = ((bf16[8,64,256]{2,1,0:T(8,128)(2,1)}), bf16[8,64,256]{2,1,0:T(8,128)(2,1)S(1)}, u32[]{:S(2)}, u32[]{:S(2)}) async-start(bf16[8,64,256]{2,1,0:T(8,128)(2,1)} %get-tuple-element.85), calls=%async_computation.4 | async-start | bytes 524288 | tf_op jit(solution)/shard_map/all_to_all | solution.py:33
  133.4 1.0 copy-start.1

commit v2 on v1

--- a/solution.py
+++ b/solution.py
@@ -74,25 +74,24 @@
     return copies
 
 
-def chunked(source, held):
-    rows = held.shape[0] // CHUNKS
-    return [(source.at[pl.ds(k * rows, rows)], held.at[pl.ds(k * rows, rows)]) for k in range(CHUNKS)]
-
-
-def streamed(sides, held, side_copy, copies):
-    rows = held.shape[0] // CHUNKS
-    side_copy.wait()
+def stage_kernel(source_ref, out_ref, sem):
+    start_copies([(source_ref, out_ref)], sem)[0].wait()
+
+
+def dense_kernel(sides_ref, inverse_ref, out_ref, sides, inverse, sem):
+    rows = inverse.shape[0] // CHUNKS
+    cuts = [pl.ds(k * rows, rows) for k in range(CHUNKS)]
+    copies = start_copies(
+        [(sides_ref, sides)] + [(inverse_ref.at[cut], inverse.at[cut]) for cut in cuts], sem
+    )
+    copies[0].wait()
     total = None
     for k in range(CHUNKS):
-        copies[k].wait()
-        part = times(sides[:, k * rows : (k + 1) * rows], held[k * rows : (k + 1) * rows])
+        copies[k + 1].wait()
+        cut = slice(k * rows, (k + 1) * rows)
+        part = times(sides[:, cut], inverse[cut])
         total = part if total is None else total + part
-    return total
-
-
-def dense_kernel(sides_ref, inverse_ref, out_ref, sides, inverse, sem):
-    copies = start_copies([(sides_ref, sides)] + chunked(inverse_ref, inverse), sem)
-    out_ref[...] = streamed(sides, inverse, copies[0], copies[1:])
+    out_ref[...] = total
 
 
 def parts(maps_ref):
@@ -101,7 +100,7 @@
 
 
 def open_up_z_kernel(me_ref, part_ref, other_ref, maps_ref, own_ref, slots_ref):
-    p, q = parts(maps_ref)[:2]
+    p, q = parts(maps_ref)
     own = (part_ref[...] + times(other_ref[...], q)).astype(BF16)
     own_ref[...] = own
     for k in range(4):
@@ -111,12 +110,12 @@
 
 def prepare_up_z_kernel(far_ref, own_ref, maps_ref, base_ref, mix_ref, far, sem):
     copies = start_copies([(far_ref, far)], sem)
-    p, q = parts(maps_ref)[:2]
+    p, q = parts(maps_ref)
     base_ref[...] = times(own_ref[...], product(p, p))
     mix_ref[0] = product(q, p)
     mix_ref[1] = q
     copies[0].wait()
-    mix_ref[2] = product(far[...], q)
+    mix_ref[2] = product(parts(far)[1], q)
 
 
 def close_up_z_kernel(me_ref, got_ref, base_ref, mix_ref, out_ref):
@@ -127,15 +126,15 @@
     out_ref[...] = total.astype(BF16)
 
 
-def settle_up_z_kernel(me_ref, got_ref, own_ref, far_ref, maps_ref, out_ref, far, sem):
+def settle_up_z_kernel(me_ref, got_ref, own_ref, far_ref, maps_ref, links_ref, out_ref, far, sem):
     copies = start_copies([(far_ref, far)], sem)
     me = me_ref[0] >> 3 & 3
-    p, q, c, k = parts(maps_ref)
+    (p, q), (c, k) = parts(maps_ref), parts(links_ref)
     own, near = own_ref[...], got_ref[me ^ 1]
     out_ref[0] = (times(near, c) + times(own, k)).astype(BF16)
     middle = (times(own, p) + times(near, q)).astype(BF16)
     copies[0].wait()
-    across = (got_ref[me ^ 2].astype(F32) + times(got_ref[me ^ 3], far[...])).astype(BF16)
+    across = (got_ref[me ^ 2].astype(F32) + times(got_ref[me ^ 3], parts(far)[1])).astype(BF16)
     out_ref[1] = (times(across, c) + times(middle, k)).astype(BF16)
 
 
@@ -146,9 +145,9 @@
         slots_ref[k] = own
 
 
-def eighth_kernel(far_ref, maps_ref, out_ref, far, sem):
+def eighth_kernel(far_ref, maps_ref, links_ref, out_ref, far, sem):
     copies = start_copies([(far_ref, far)], sem)
-    p, q, c, k = parts(maps_ref)
+    (p, q), (c, k) = parts(maps_ref), parts(links_ref)
     copies[0].wait()
     far_p, far_q = parts(far)
     eight, far_eight = {0: p, 1: q}, {2: far_p, 3: far_q}
@@ -162,9 +161,11 @@
         out_ref[j] = total.astype(BF16)
 
 
-def prepare_top_kernel(near_ref, eighth_ref, own_ref, maps_ref, base_ref, mix_ref, near, eighth, sem):
+def prepare_top_kernel(
+    near_ref, eighth_ref, own_ref, maps_ref, links_ref, base_ref, mix_ref, near, eighth, sem
+):
     copies = start_copies([(near_ref, near), (eighth_ref, eighth)], sem)
-    p, q, c, k = parts(maps_ref)
+    (p, q), (c, k) = parts(maps_ref), parts(links_ref)
     for copy in copies:
         copy.wait()
     for j in range(4):
@@ -199,7 +200,7 @@
 
 def prepare_down_kernel(far_ref, own_ref, local_ref, maps_ref, base_ref, mix_ref, far, sem):
     copies = start_copies([(far_ref, far)], sem)
-    p, q = parts(maps_ref)[:2]
+    p, q = parts(maps_ref)
     base_ref[...] = times_t(own_ref[...], p) + local_ref[...].astype(F32)
     mix_ref[0] = q
     mix_ref[1] = product(p, q)
@@ -211,7 +212,7 @@
     (core_ref, y1_ref, cy_ref, dense_ref, own_ref, one_ref, two_ref, maps_ref, basis_ref) = refs[:9]
     base_ref, mix_ref, core, y1, cy, dense, sem = refs[9:]
     copies = start_copies([(core_ref, core), (y1_ref, y1), (cy_ref, cy), (dense_ref, dense)], sem)
-    p, q = parts(maps_ref)[:2]
+    p, q = parts(maps_ref)
     mix = [product(p, p), None, product(p, q), None]
     for copy in copies:
         copy.wait()
@@ -253,6 +254,9 @@
         prefetched[name] = swap(value, mask)
 
     current = times(right_sides, leaf_basis).astype(BF16)
+    held = [pltpu.SemaphoreType.DMA((1,))]
+    outs = [(transfer.shape, BF16)]
+    (transfer,) = call(stage_kernel, outs, [after(transfer, current)], [IN_HBM], held)
     own_map, other_map = transfer[:rank], transfer[rank:]
     from_other, from_own = coupling[:rank], coupling[rank:]
 
@@ -261,6 +265,8 @@
         total = times(far, from_other) + times(own, from_own)
         local[level] = lax.optimization_barrier(total.astype(BF16))
 
+    late = []
+
     def half_up(current, bit):
         other = swap(current, 1 << bit)
         part = times(current, own_map)
@@ -269,69 +275,85 @@
     def up(current, bit):
         part, other = half_up(current, bit)
         above = (part + times(other, other_map)).astype(BF16)
-        settle(bit + 1, other, current, above)
+        late.append((bit + 1, other, current))
         return above
 
     current = up(current, 0)
-    maps = jnp.concatenate(after((transfer, coupling), current), 0)
-    prefetch("pre_q_z2", after(transfer, current)[rank:], 16, current)
+    prefetch("pre_z2", transfer, 16, current)
     current = up(current, 1)
-    prefetch("pre_x2", transfer, 256, current)
+    copied = [right_sides, leaf_inverse]
+    (dense,) = call(
+        dense_kernel,
+        [((columns, leaf_inverse.shape[1]), F32)],
+        [after(right_sides, current), leaf_inverse],
+        [IN_HBM] * 2,
+        [pltpu.VMEM(a.shape, a.dtype) for a in copied] + [pltpu.SemaphoreType.DMA((CHUNKS + 1,))],
+        None,
+    )
     below = current
     part, other = half_up(below, 2)
 
     current, slots = call(
         open_up_z_kernel,
         [(block, BF16), ((4, *block), BF16)],
-        [me, part, other, maps],
+        [me, part, other, transfer],
         [IN_SMEM] + [IN_VMEM] * 3,
     )
-    settle(3, other, below, current)
+    late.append((3, other, below))
+    prefetch("pre_x2", transfer, 256, slots)
+    got = exchange(slots, 3, 2)
+    far = prefetched["pre_z2"]
+    base, mix = call(
+        prepare_up_z_kernel,
+        [(block, F32), ((3, *square), BF16)],
+        [far, current, transfer],
+        [IN_HBM] + [IN_VMEM] * 2,
+        fetched([far]),
+    )
+    below = current
+    (current,) = call(
+        close_up_z_kernel, [(block, BF16)], [me, got, base, mix], [IN_SMEM] + [IN_VMEM] * 3
+    )
+    (settled,) = call(
+        settle_up_z_kernel,
+        [((2, *block), BF16)],
+        [me, got, after(below, current), far, transfer, coupling],
+        [IN_SMEM, IN_VMEM, IN_VMEM, IN_HBM, IN_VMEM, IN_VMEM],
+        fetched([far]),
+    )
     far = prefetched["pre_x2"]
     (eighth,) = call(
         eighth_kernel,
         [((4, *square), BF16)],
-        [far, after(maps, slots)],
-        [IN_HBM, IN_VMEM],
+        [far, after(transfer, current), coupling],
+        [IN_HBM, IN_VMEM, IN_VMEM],
         fetched([far]),
     )
-    prefetch("pre_x1", eighth, 128, slots)
-    got = exchange(slots, 3, 2)
-    far = prefetched["pre_q_z2"]
-    base, mix = call(
-        prepare_up_z_kernel,
-        [(block, F32), ((3, *square), BF16)],
-        [far, current, maps],
-        [IN_HBM] + [IN_VMEM] * 2,
-        fetched([far]),
-    )
-    below = current
-    (current,) = call(
-        close_up_z_kernel, [(block, BF16)], [me, got, base, mix], [IN_SMEM] + [IN_VMEM] * 3
-    )
-    (settled,) = call(
-        settle_up_z_kernel,
-        [((2, *block), BF16)],
-        [me, got, after(below, current), far, maps],
-        [IN_SMEM, IN_VMEM, IN_VMEM, IN_HBM, IN_VMEM],
-        fetched([far]),
-    )
+    for level, far_t, own_t in late:
+        settle(level, far_t, own_t, current)
+    late.clear()
     current = up(current, 5)
+    prefetch("pre_x1", eighth, 128, current)
+    prefetch("pre_q_z4", after(transfer, current)[rank:], 32, current)
     below = current
     part, other = half_up(below, 6)
 
     current, slots = call(
-        open_top_kernel, [(block, BF16), ((4, *block), BF16)], [part, other, maps], [IN_VMEM] * 3
+        open_top_kernel,
+        [(block, BF16), ((4, *block), BF16)],
+        [part, other, transfer],
+        [IN_VMEM] * 3,
     )
     settle(7, other, below, current)
-    prefetch("pre_q_z4", after(transfer, slots)[rank:], 32, slots)
+    for level, far_t, own_t in late:
+        settle(level, far_t, own_t, slots)
     got = exchange(slots, 7, 2)
     near = prefetched["pre_x1"]
     base, mix = call(
         prepare_top_kernel,
         [(block, F32), ((3, *square), BF16)],
-        [near, eighth, current, maps],
-        [IN_HBM] * 2 + [IN_VMEM] * 2,
+        [near, eighth, current, transfer, coupling],
+        [IN_HBM] * 2 + [IN_VMEM] * 3,
         fetched([near, eighth]),
     )
     local[4], local[5] = settled[0], settled[1]
@@ -340,7 +362,7 @@
         return call(
             kernel,
             [(block, BF16), ((1 << width, *block), BF16)],
-            [me, got, base, mix, local[level], maps],
+            [me, got, base, mix, local[level], transfer],
             [IN_SMEM] + [IN_VMEM] * 5,
         )
 
@@ -348,7 +370,7 @@
         return call(
             prepare_down_kernel,
             [(block, F32), ((3, *square), BF16)],
-            [far, own, local[level], maps],
+            [far, own, local[level], transfer],
             [IN_HBM] + [IN_VMEM] * 3,
             fetched([far]),
         )
@@ -362,26 +384,17 @@
     base, mix = prepare_down(prefetched["pre_q_z4"], own, 6)
 
     own, slots = turn_down(turn(5, times_t, 3, 2), got, base, mix, 5, 2)
-    prefetch("pre_core", jnp.concatenate(after((maps[: 2 * rank], local[2]), slots), 0), 1, slots)
+    prefetch("pre_core", jnp.concatenate(after((transfer, local[2]), slots), 0), 1, slots)
     got = exchange(slots, 3, 2)
     base, mix = prepare_down(prefetched["pre_q_z1"], own, 4)
 
     own, slots = turn_down(turn(3, times_t, 0, 3), got, base, mix, 3, 3)
     got = exchange(slots, 0, 3)
-    copied = [right_sides, leaf_inverse]
-    (dense,) = call(
-        dense_kernel,
-        [((columns, leaf_inverse.shape[1]), F32)],
-        [after(right_sides, slots), leaf_inverse],
-        [IN_HBM] * 2,
-        [pltpu.VMEM(a.shape, a.dtype) for a in copied] + [pltpu.SemaphoreType.DMA((CHUNKS + 1,))],
-        None,
-    )
     near = [prefetched[f"pre_{name}"] for name in ("core", "q_y1", "q_cy")]
     base, mix = call(
         prepare_down_y_kernel,
         [(dense.shape, F32), ((7, *square), BF16)],
-        [*near, dense, own, local[1], local[2], maps, leaf_basis],
+        [*near, dense, own, local[1], local[2], transfer, leaf_basis],
         [IN_HBM] * 4 + [IN_VMEM] * 5,
         fetched([*near, dense]),
     )

time: 140 us -> 138 us (0.986)
  waiting for transfers between devices: 22.3 us -> 36.3 us
  starting transfers between devices: 90.2 us -> 80.7 us
  matrix products: 7.58 us -> 3.92 us
  local copies, waits for them, and re-layouts: 2.93 us -> 1.01 us
    all_to_all x5, waiting for transfers between devices: 4.88 us -> 19.7 us  [exchange(): return lax.all_to_all(slots, AXIS, 0, 0, axis_index_groups=groups)]
    ppermute x13, starting transfers between devices: 64.2 us -> 58.6 us  [swap(): return lax.ppermute(block, AXIS, route)]
    all_to_all x5, starting transfers between devices: 26.1 us -> 22.1 us  [exchange(): return lax.all_to_all(slots, AXIS, 0, 0, axis_index_groups=groups)]
    dot_general x19, matrix products: 7.58 us -> 3.92 us  [times(): return jnp.dot(values, matrix, preferred_element_type=F32)]
    pallas_call x15 -> x16, Pallas kernels: 15.3 us -> 15 us  [call(): pl.pallas_call(kernel, out_shape=outs, in_specs=specs, out_specs=[IN_VMEM...]
  transfers between devices with their start and end apart: 18 -> 18, of which waited for: 6 -> 8; matrix products, arithmetic and copies ran while one was open for 5% -> 2% of each run, Pallas kernels for 8% -> 8%
where the time goes in v2:
time: 138 us; the launch traced here: 137 us
  starting transfers between devices  80.7 us (58%)
  waiting for transfers between devices  36.3 us (26%)
  Pallas kernels  15 us (11%)
  matrix products  3.92 us (3%)
    ppermute x13, starting transfers between devices, swap(): return lax.ppermute(block, AXIS, route)  58.6 us
    all_to_all x5, starting transfers between devices, exchange(): return lax.all_to_all(slots, AXIS, 0, 0, axis_index_groups=groups)  22.1 us
    all_to_all x5, waiting for transfers between devices, exchange(): return lax.all_to_all(slots, AXIS, 0, 0, axis_index_groups=groups)  19.7 us
    ppermute x13, waiting for transfers between devices, swap(): return lax.ppermute(block, AXIS, route)  16.6 us
    pallas_call x16, Pallas kernels, call(): pl.pallas_call(kernel, out_shape=outs, in_specs=specs, out_specs=[IN_VMEM...  15 us
    dot_general x19, matrix products, times(): return jnp.dot(values, matrix, preferred_element_type=F32)  3.92 us
  transfers between devices with their start and end apart: 18, of which 8 were waited for; matrix products, arithmetic and copies ran while one was open for 2% of the time, Pallas kernels for 8%

profile of v2, /device:TPU:1, one launch (start us, length us, event | category | flops | bytes accessed | tf_op | source)
XLA Modules:
  0.0 137.3 jit_solution(8503688396362402175)
XLA Ops:
  0.0 1.3 convolution_convert_fusion
  1.3 8.7 %collective-permute-start = (bf16[64,256]{1,0:T(8,128)(2,1)S(1)}, bf16[64,256]{1,0:T(8,128)(2,1)S(1)}, u32[]{:S(2)}, u32[]{:S(2)}) collective-permute-start(bf16[64,256]{1,0:T(8,128)(2,1)S(1)} %convolution_convert_fusion), channel_id=1, source_target_pairs={{0,1},{1,0},{2,3},{3,2},{4,5},{5,4},{6,7},{7,6},{8,9},{9,8},{10,11... | collective-permute-start | bytes 98312 | tf_op jit(solution)/shard_map/ppermute | solution.py:23
  11.4 1.9 %collective-permute-start.1 = (bf16[64,256]{1,0:T(8,128)(2,1)S(1)}, bf16[64,256]{1,0:T(8,128)(2,1)S(1)}, u32[]{:S(2)}, u32[]{:S(2)}) collective-permute-start(bf16[64,256]{1,0:T(8,128)(2,1)S(1)} %fusion), channel_id=1, source_target_pairs={{0,2},{1,3},{2,0},{3,1},{4,6},{5,7},{6,4},{7,5},{8,10},{9,11},{10,... | collective-permute-start | bytes 98312 | tf_op jit(solution)/shard_map/ppermute | solution.py:23
  13.4 2.6 %collective-permute-done.1 = bf16[64,256]{1,0:T(8,128)(2,1)S(1)} collective-permute-done((bf16[64,256]{1,0:T(8,128)(2,1)S(1)}, bf16[64,256]{1,0:T(8,128)(2,1)S(1)}, u32[]{:S(2)}, u32[]{:S(2)}) %collective-permute-start.1) | collective-permute-done | bytes 32800 | tf_op jit(solution)/shard_map/ppermute | solution.py:23
  16.2 1.9 %collective-permute-start.2 = (bf16[64,256]{1,0:T(8,128)(2,1)S(1)}, bf16[64,256]{1,0:T(8,128)(2,1)S(1)}, u32[]{:S(2)}, u32[]{:S(2)}) collective-permute-start(bf16[64,256]{1,0:T(8,128)(2,1)S(1)} %fusion.1), channel_id=1, source_target_pairs={{0,4},{1,5},{2,6},{3,7},{4,0},{5,1},{6,2},{7,3},{8,12},{9,13},{10,... | collective-permute-start | bytes 98312 | tf_op jit(solution)/shard_map/ppermute | solution.py:23
  18.2 4.1 %collective-permute-done.2.other_ref = bf16[64,256]{1,0:T(8,128)(2,1)S(1)} collective-permute-done((bf16[64,256]{1,0:T(8,128)(2,1)S(1)}, bf16[64,256]{1,0:T(8,128)(2,1)S(1)}, u32[]{:S(2)}, u32[]{:S(2)}) %collective-permute-start.2) | collective-permute-done | bytes 32800 | tf_op jit(solution)/shard_map/ppermute | solution.py:23
  23.3 3.3 %all-to-all-start = ((bf16[4,64,256]{2,1,0:T(8,128)(2,1)}), bf16[4,64,256]{2,1,0:T(8,128)(2,1)S(1)}, u32[]{:S(2)}, u32[]{:S(2)}) async-start(bf16[4,64,256]{2,1,0:T(8,128)(2,1)} %get-tuple-element.50), calls=%async_computation | async-start | bytes 262144 | tf_op jit(solution)/shard_map/all_to_all | solution.py:33
  26.6 4.2 %collective-permute-start.3 = (bf16[512,256]{1,0:T(8,128)(2,1)S(1)}, bf16[512,256]{1,0:T(8,128)(2,1)S(1)}, u32[]{:S(2)}, u32[]{:S(2)}) collective-permute-start(bf16[512,256]{1,0:T(8,128)(2,1)S(1)} %shard_map.55.maps_ref.refs_7_), channel_id=1, source_target_pairs={{0,16},{1,17},{2,18},{3,19},{4,20},{5,21},{6,22},{7,23},{8,24},{9,... | collective-permute-start | bytes 786440 | tf_op jit(solution)/shard_map/ppermute | solution.py:23
  30.8 2.5 %shard_map.68.refs_3_ = f32[64,1024]{1,0:T(8,128)} custom-call(bf16[64,1024]{1,0:T(8,128)(2,1)} %sides_ref, bf16[1024,1024]{1,0:T(8,128)(2,1)} %inverse_ref.1), custom_call_target="tpu_custom_call" | custom-call | tf_op jit(solution)/shard_map/pallas_call | solution.py:53
  33.4 1.9 %collective-permute-start.6 = (bf16[512,256]{1,0:T(8,128)(2,1)S(1)}, bf16[512,256]{1,0:T(8,128)(2,1)S(1)}, u32[]{:S(2)}, u32[]{:S(2)}) collective-permute-start(bf16[512,256]{1,0:T(8,128)(2,1)S(1)} %shard_map.55.maps_ref.refs_7_), channel_id=1, source_target_pairs={{0,256},{1,257},{2,258},{3,259},{4,260},{5,261},{6,262},{7,263},{8... | collective-permute-start | bytes 786440 | tf_op jit(solution)/shard_map/ppermute | solution.py:23
  35.3 8.1 %collective-permute-done.3.far_ref = bf16[512,256]{1,0:T(8,128)(2,1)S(1)} collective-permute-done((bf16[512,256]{1,0:T(8,128)(2,1)S(1)}, bf16[512,256]{1,0:T(8,128)(2,1)S(1)}, u32[]{:S(2)}, u32[]{:S(2)}) %collective-permute-start.3) | collective-permute-done | bytes 262176 | tf_op jit(solution)/shard_map/ppermute | solution.py:23
  44.3 5.6 %collective-permute-start.4 = (bf16[64,256]{1,0:T(8,128)(2,1)S(1)}, bf16[64,256]{1,0:T(8,128)(2,1)S(1)}, u32[]{:S(2)}, u32[]{:S(2)}) collective-permute-start(bf16[64,256]{1,0:T(8,128)(2,1)S(1)} %shard_map.58), channel_id=1, source_target_pairs={{0,32},{1,33},{2,34},{3,35},{4,36},{5,37},{6,38},{7,39},{8,40},{9,... | collective-permute-start | bytes 98312 | tf_op jit(solution)/shard_map/ppermute | solution.py:23
  52.0 1.2 collective-permute-done.4
  53.5 10.1 %collective-permute-start.5 = (bf16[64,256]{1,0:T(8,128)(2,1)S(1)}, bf16[64,256]{1,0:T(8,128)(2,1)S(1)}, u32[]{:S(2)}, u32[]{:S(2)}) collective-permute-start(bf16[64,256]{1,0:T(8,128)(2,1)S(1)} %fusion.2), channel_id=1, source_target_pairs={{0,64},{1,65},{2,66},{3,67},{4,68},{5,69},{6,70},{7,71},{8,72},{9,... | collective-permute-start | bytes 98312 | tf_op jit(solution)/shard_map/ppermute | solution.py:23
  63.7 3.1 %collective-permute-start.7 = (bf16[4,256,256]{2,1,0:T(8,128)(2,1)S(1)}, bf16[4,256,256]{2,1,0:T(8,128)(2,1)S(1)}, u32[]{:S(2)}, u32[]{:S(2)}) collective-permute-start(bf16[4,256,256]{2,1,0:T(8,128)(2,1)S(1)} %shard_map.60.eighth_ref), channel_id=1, source_target_pairs={{0,128},{1,129},{2,130},{3,131},{4,132},{5,133},{6,134},{7,135},{8... | collective-permute-start | bytes 1572872 | tf_op jit(solution)/shard_map/ppermute | solution.py:23
  66.9 3.7 %collective-permute-start.8 = (bf16[256,256]{1,0:T(8,128)(2,1)S(1)}, bf16[256,256]{1,0:T(8,128)(2,1)S(1)}, u32[]{:S(2)}, u32[]{:S(2)}) collective-permute-start(bf16[256,256]{1,0:T(8,128)(2,1)S(1)} %slice.28), channel_id=1, source_target_pairs={{0,32},{1,33},{2,34},{3,35},{4,36},{5,37},{6,38},{7,39},{8,40},{9,... | collective-permute-start | bytes 393224 | tf_op jit(solution)/shard_map/ppermute | solution.py:23
  71.5 3.7 %all-to-all-start.1 = ((bf16[4,64,256]{2,1,0:T(8,128)(2,1)}), bf16[4,64,256]{2,1,0:T(8,128)(2,1)S(1)}, u32[]{:S(2)}, u32[]{:S(2)}) async-start(bf16[4,64,256]{2,1,0:T(8,128)(2,1)} %get-tuple-element.55), calls=%async_computation.1 | async-start | bytes 262144 | tf_op jit(solution)/shard_map/all_to_all | solution.py:33
  76.9 3.8 %all-to-all-done.1.got_ref = bf16[4,64,256]{2,1,0:T(8,128)(2,1)S(1)} async-done(((bf16[4,64,256]{2,1,0:T(8,128)(2,1)}), bf16[4,64,256]{2,1,0:T(8,128)(2,1)S(1)}, u32[]{:S(2)}, u32[]{:S(2)}) %all-to-all-start.1) | async-done | bytes 131104 | tf_op jit(solution)/shard_map/all_to_all | solution.py:33
  80.7 1.0 shard_map.62
  81.7 6.0 %all-to-all-start.2 = ((bf16[4,64,256]{2,1,0:T(8,128)(2,1)}), bf16[4,64,256]{2,1,0:T(8,128)(2,1)S(1)}, u32[]{:S(2)}, u32[]{:S(2)}) async-start(bf16[4,64,256]{2,1,0:T(8,128)(2,1)} %get-tuple-element.64), calls=%async_computation.2 | async-start | bytes 262144 | tf_op jit(solution)/shard_map/all_to_all | solution.py:33
  88.7 11.1 %all-to-all-done.2.got_ref = bf16[4,64,256]{2,1,0:T(8,128)(2,1)S(1)} async-done(((bf16[4,64,256]{2,1,0:T(8,128)(2,1)}), bf16[4,64,256]{2,1,0:T(8,128)(2,1)S(1)}, u32[]{:S(2)}, u32[]{:S(2)}) %all-to-all-start.2) | async-done | bytes 131104 | tf_op jit(solution)/shard_map/all_to_all | solution.py:33
  99.8 1.1 shard_map.65
  100.8 3.8 %all-to-all-start.3 = ((bf16[4,64,256]{2,1,0:T(8,128)(2,1)}), bf16[4,64,256]{2,1,0:T(8,128)(2,1)S(1)}, u32[]{:S(2)}, u32[]{:S(2)}) async-start(bf16[4,64,256]{2,1,0:T(8,128)(2,1)} %get-tuple-element.73), calls=%async_computation.3 | async-start | bytes 262144 | tf_op jit(solution)/shard_map/all_to_all | solution.py:33
  104.9 3.4 %collective-permute-start.9 = (bf16[256,256]{1,0:T(8,128)(2,1)S(1)}, bf16[256,256]{1,0:T(8,128)(2,1)S(1)}, u32[]{:S(2)}, u32[]{:S(2)}) collective-permute-start(bf16[256,256]{1,0:T(8,128)(2,1)S(1)} %slice.30), channel_id=1, source_target_pairs={{0,8},{1,9},{2,10},{3,11},{4,12},{5,13},{6,14},{7,15},{8,0},{9,1},... | collective-permute-start | bytes 393224 | tf_op jit(solution)/shard_map/ppermute | solution.py:23
  108.3 8.7 %collective-permute-start.10 = (bf16[576,256]{1,0:T(8,128)(2,1)S(1)}, bf16[576,256]{1,0:T(8,128)(2,1)S(1)}, u32[]{:S(2)}, u32[]{:S(2)}) collective-permute-start(bf16[576,256]{1,0:T(8,128)(2,1)S(1)} %pad_maximum_fusion), channel_id=1, source_target_pairs={{0,1},{1,0},{2,3},{3,2},{4,5},{5,4},{6,7},{7,6},{8,9},{9,8},{10,11... | collective-permute-start | bytes 884744 | tf_op jit(solution)/shard_map/ppermute | solution.py:23
  117.2 3.1 %collective-permute-start.12 = (bf16[256,256]{1,0:T(8,128)(2,1)S(1)}, bf16[256,256]{1,0:T(8,128)(2,1)S(1)}, u32[]{:S(2)}, u32[]{:S(2)}) collective-permute-start(bf16[256,256]{1,0:T(8,128)(2,1)S(1)} %slice.30), channel_id=1, source_target_pairs={{0,3},{1,2},{2,1},{3,0},{4,7},{5,6},{6,5},{7,4},{8,11},{9,10},{10,... | collective-permute-start | bytes 393224 | tf_op jit(solution)/shard_map/ppermute | solution.py:23
  120.3 2.1 %collective-permute-start.11 = (bf16[256,256]{1,0:T(8,128)(2,1)S(1)}, bf16[256,256]{1,0:T(8,128)(2,1)S(1)}, u32[]{:S(2)}, u32[]{:S(2)}) collective-permute-start(bf16[256,256]{1,0:T(8,128)(2,1)S(1)} %slice.30), channel_id=1, source_target_pairs={{0,2},{1,3},{2,0},{3,1},{4,6},{5,7},{6,4},{7,5},{8,10},{9,11},{10,... | collective-permute-start | bytes 393224 | tf_op jit(solution)/shard_map/ppermute | solution.py:23
  123.0 1.1 shard_map.67
  124.1 5.2 %all-to-all-start.4 = ((bf16[8,64,256]{2,1,0:T(8,128)(2,1)}), bf16[8,64,256]{2,1,0:T(8,128)(2,1)S(1)}, u32[]{:S(2)}, u32[]{:S(2)}) async-start(bf16[8,64,256]{2,1,0:T(8,128)(2,1)} %get-tuple-element.81), calls=%async_computation.4 | async-start | bytes 524288 | tf_op jit(solution)/shard_map/all_to_all | solution.py:33
  129.5 1.5 %shard_map.69 = (f32[64,1024]{1,0:T(8,128)S(1)}, bf16[7,256,256]{2,1,0:T(8,128)(2,1)S(1)}) custom-call(bf16[576,256]{1,0:T(8,128)(2,1)S(1)} %collective-permute-done.10.refs_0_, bf16[256,256]{1,0:T(8,128)(2,1)S(1)} %collective-permute-done.11.refs_1_, bf16[256,256]{1,0:T(8,128)(2,1)S(1)} %collective-permute-done.12.refs_2_, f32[64,1024]{1,0:T(8,128)S(1)} %copy-done.2, ...), custom_call_target="tpu_custom_call" | custom-call | tf_op jit(solution)/shard_map/pallas_call | solution.py:53
  131.1 4.7 %all-to-all-done.4.got_ref = bf16[8,64,256]{2,1,0:T(8,128)(2,1)S(1)} async-done(((bf16[8,64,256]{2,1,0:T(8,128)(2,1)}), bf16[8,64,256]{2,1,0:T(8,128)(2,1)S(1)}, u32[]{:S(2)}, u32[]{:S(2)}) %all-to-all-start.4) | async-done | bytes 262176 | tf_op jit(solution)/shard_map/all_to_all | solution.py:33
  135.8 1.5 %shard_map.70 = bf16[64,1024]{1,0:T(8,128)(2,1)} custom-call(s32[1]{0:T(128)} %bitcast.me_ref, bf16[8,64,256]{2,1,0:T(8,128)(2,1)S(1)} %all-to-all-done.4.got_ref, f32[64,1024]{1,0:T(8,128)S(1)} %get-tuple-element.91.base_ref, bf16[7,256,256]{2,1,0:T(8,128)(2,1)S(1)} %get-tuple-element.92.mix_ref, bf16[1024,256]{1,0:T(8,128)(2,1)S(1)} %copy-done.1), custom_call_target="tpu_custom_call" | custom-call | tf_op jit(solution)/shard_map/pallas_call | solution.py:53
  (51 shorter events, 10.4 us)
Async XLA Ops:
  1.3 9.9 %collective-permute-start = (bf16[64,256]{1,0:T(8,128)(2,1)S(1)}, bf16[64,256]{1,0:T(8,128)(2,1)S(1)}, u32[]{:S(2)}, u32[]{:S(2)}) collective-permute-start(bf16[64,256]{1,0:T(8,128)(2,1)S(1)} %convolution_convert_fusion), channel_id=1, source_target_pairs={{0,1},{1,0},{2,3},{3,2},{4,5},{5,4},{6,7},{7,6},{8,9},{9,8},{10,11... | collective-permute-start | bytes 98312 | tf_op jit(solution)/shard_map/ppermute | solution.py:23
  10.1 1.0 copy-start.3
  11.4 4.7 %collective-permute-start.1 = (bf16[64,256]{1,0:T(8,128)(2,1)S(1)}, bf16[64,256]{1,0:T(8,128)(2,1)S(1)}, u32[]{:S(2)}, u32[]{:S(2)}) collective-permute-start(bf16[64,256]{1,0:T(8,128)(2,1)S(1)} %fusion), channel_id=1, source_target_pairs={{0,2},{1,3},{2,0},{3,1},{4,6},{5,7},{6,4},{7,5},{8,10},{9,11},{10,... | collective-permute-start | bytes 98312 | tf_op jit(solution)/shard_map/ppermute | solution.py:23
  16.2 6.2 %collective-permute-start.2 = (bf16[64,256]{1,0:T(8,128)(2,1)S(1)}, bf16[64,256]{1,0:T(8,128)(2,1)S(1)}, u32[]{:S(2)}, u32[]{:S(2)}) collective-permute-start(bf16[64,256]{1,0:T(8,128)(2,1)S(1)} %fusion.1), channel_id=1, source_target_pairs={{0,4},{1,5},{2,6},{3,7},{4,0},{5,1},{6,2},{7,3},{8,12},{9,13},{10,... | collective-permute-start | bytes 98312 | tf_op jit(solution)/shard_map/ppermute | solution.py:23
  22.3 27.6 %copy-start = (bf16[512,256]{1,0:T(8,128)(2,1)S(1)}, bf16[512,256]{1,0:T(8,128)(2,1)}, u32[]{:S(2)}) copy-start(bf16[512,256]{1,0:T(8,128)(2,1)} %links_ref.5) | copy-start | bytes 786436
  23.3 20.8 %all-to-all-start = ((bf16[4,64,256]{2,1,0:T(8,128)(2,1)}), bf16[4,64,256]{2,1,0:T(8,128)(2,1)S(1)}, u32[]{:S(2)}, u32[]{:S(2)}) async-start(bf16[4,64,256]{2,1,0:T(8,128)(2,1)} %get-tuple-element.50), calls=%async_computation | async-start | bytes 262144 | tf_op jit(solution)/shard_map/all_to_all | solution.py:33
  26.6 16.8 %collective-permute-start.3 = (bf16[512,256]{1,0:T(8,128)(2,1)S(1)}, bf16[512,256]{1,0:T(8,128)(2,1)S(1)}, u32[]{:S(2)}, u32[]{:S(2)}) collective-permute-start(bf16[512,256]{1,0:T(8,128)(2,1)S(1)} %shard_map.55.maps_ref.refs_7_), channel_id=1, source_target_pairs={{0,16},{1,17},{2,18},{3,19},{4,20},{5,21},{6,22},{7,23},{8,24},{9,... | collective-permute-start | bytes 786440 | tf_op jit(solution)/shard_map/ppermute | solution.py:23
  33.4 17.6 %collective-permute-start.6 = (bf16[512,256]{1,0:T(8,128)(2,1)S(1)}, bf16[512,256]{1,0:T(8,128)(2,1)S(1)}, u32[]{:S(2)}, u32[]{:S(2)}) collective-permute-start(bf16[512,256]{1,0:T(8,128)(2,1)S(1)} %shard_map.55.maps_ref.refs_7_), channel_id=1, source_target_pairs={{0,256},{1,257},{2,258},{3,259},{4,260},{5,261},{6,262},{7,263},{8... | collective-permute-start | bytes 786440 | tf_op jit(solution)/shard_map/ppermute | solution.py:23
  44.3 8.9 %collective-permute-start.4 = (bf16[64,256]{1,0:T(8,128)(2,1)S(1)}, bf16[64,256]{1,0:T(8,128)(2,1)S(1)}, u32[]{:S(2)}, u32[]{:S(2)}) collective-permute-start(bf16[64,256]{1,0:T(8,128)(2,1)S(1)} %shard_map.58), channel_id=1, source_target_pairs={{0,32},{1,33},{2,34},{3,35},{4,36},{5,37},{6,38},{7,39},{8,40},{9,... | collective-permute-start | bytes 98312 | tf_op jit(solution)/shard_map/ppermute | solution.py:23
  53.5 17.1 %collective-permute-start.5 = (bf16[64,256]{1,0:T(8,128)(2,1)S(1)}, bf16[64,256]{1,0:T(8,128)(2,1)S(1)}, u32[]{:S(2)}, u32[]{:S(2)}) collective-permute-start(bf16[64,256]{1,0:T(8,128)(2,1)S(1)} %fusion.2), channel_id=1, source_target_pairs={{0,64},{1,65},{2,66},{3,67},{4,68},{5,69},{6,70},{7,71},{8,72},{9,... | collective-permute-start | bytes 98312 | tf_op jit(solution)/shard_map/ppermute | solution.py:23
  63.7 12.4 %collective-permute-start.7 = (bf16[4,256,256]{2,1,0:T(8,128)(2,1)S(1)}, bf16[4,256,256]{2,1,0:T(8,128)(2,1)S(1)}, u32[]{:S(2)}, u32[]{:S(2)}) collective-permute-start(bf16[4,256,256]{2,1,0:T(8,128)(2,1)S(1)} %shard_map.60.eighth_ref), channel_id=1, source_target_pairs={{0,128},{1,129},{2,130},{3,131},{4,132},{5,133},{6,134},{7,135},{8... | collective-permute-start | bytes 1572872 | tf_op jit(solution)/shard_map/ppermute | solution.py:23
  66.9 21.1 %collective-permute-start.8 = (bf16[256,256]{1,0:T(8,128)(2,1)S(1)}, bf16[256,256]{1,0:T(8,128)(2,1)S(1)}, u32[]{:S(2)}, u32[]{:S(2)}) collective-permute-start(bf16[256,256]{1,0:T(8,128)(2,1)S(1)} %slice.28), channel_id=1, source_target_pairs={{0,32},{1,33},{2,34},{3,35},{4,36},{5,37},{6,38},{7,39},{8,40},{9,... | collective-permute-start | bytes 393224 | tf_op jit(solution)/shard_map/ppermute | solution.py:23
  71.5 9.2 %all-to-all-start.1 = ((bf16[4,64,256]{2,1,0:T(8,128)(2,1)}), bf16[4,64,256]{2,1,0:T(8,128)(2,1)S(1)}, u32[]{:S(2)}, u32[]{:S(2)}) async-start(bf16[4,64,256]{2,1,0:T(8,128)(2,1)} %get-tuple-element.55), calls=%async_computation.1 | async-start | bytes 262144 | tf_op jit(solution)/shard_map/all_to_all | solution.py:33
  81.7 18.0 %all-to-all-start.2 = ((bf16[4,64,256]{2,1,0:T(8,128)(2,1)}), bf16[4,64,256]{2,1,0:T(8,128)(2,1)S(1)}, u32[]{:S(2)}, u32[]{:S(2)}) async-start(bf16[4,64,256]{2,1,0:T(8,128)(2,1)} %get-tuple-element.64), calls=%async_computation.2 | async-start | bytes 262144 | tf_op jit(solution)/shard_map/all_to_all | solution.py:33
  99.8 29.7 %copy-start.1 = (bf16[1024,256]{1,0:T(8,128)(2,1)S(1)}, bf16[1024,256]{1,0:T(8,128)(2,1)}, u32[]{:S(2)}) copy-start(bf16[1024,256]{1,0:T(8,128)(2,1)} %basis_ref.1) | copy-start | bytes 1572868
  99.8 29.7 %copy-start.2 = (f32[64,1024]{1,0:T(8,128)S(1)}, f32[64,1024]{1,0:T(8,128)}, u32[]{:S(2)}) copy-start(f32[64,1024]{1,0:T(8,128)} %shard_map.68.refs_3_) | copy-start | bytes 786436
  100.8 22.1 %all-to-all-start.3 = ((bf16[4,64,256]{2,1,0:T(8,128)(2,1)}), bf16[4,64,256]{2,1,0:T(8,128)(2,1)S(1)}, u32[]{:S(2)}, u32[]{:S(2)}) async-start(bf16[4,64,256]{2,1,0:T(8,128)(2,1)} %get-tuple-element.73), calls=%async_computation.3 | async-start | bytes 262144 | tf_op jit(solution)/shard_map/all_to_all | solution.py:33
  104.9 17.5 %collective-permute-start.9 = (bf16[256,256]{1,0:T(8,128)(2,1)S(1)}, bf16[256,256]{1,0:T(8,128)(2,1)S(1)}, u32[]{:S(2)}, u32[]{:S(2)}) collective-permute-start(bf16[256,256]{1,0:T(8,128)(2,1)S(1)} %slice.30), channel_id=1, source_target_pairs={{0,8},{1,9},{2,10},{3,11},{4,12},{5,13},{6,14},{7,15},{8,0},{9,1},... | collective-permute-start | bytes 393224 | tf_op jit(solution)/shard_map/ppermute | solution.py:23
  108.3 21.2 %collective-permute-start.10 = (bf16[576,256]{1,0:T(8,128)(2,1)S(1)}, bf16[576,256]{1,0:T(8,128)(2,1)S(1)}, u32[]{:S(2)}, u32[]{:S(2)}) collective-permute-start(bf16[576,256]{1,0:T(8,128)(2,1)S(1)} %pad_maximum_fusion), channel_id=1, source_target_pairs={{0,1},{1,0},{2,3},{3,2},{4,5},{5,4},{6,7},{7,6},{8,9},{9,8},{10,11... | collective-permute-start | bytes 884744 | tf_op jit(solution)/shard_map/ppermute | solution.py:23
  117.2 12.3 %collective-permute-start.12 = (bf16[256,256]{1,0:T(8,128)(2,1)S(1)}, bf16[256,256]{1,0:T(8,128)(2,1)S(1)}, u32[]{:S(2)}, u32[]{:S(2)}) collective-permute-start(bf16[256,256]{1,0:T(8,128)(2,1)S(1)} %slice.30), channel_id=1, source_target_pairs={{0,3},{1,2},{2,1},{3,0},{4,7},{5,6},{6,5},{7,4},{8,11},{9,10},{10,... | collective-permute-start | bytes 393224 | tf_op jit(solution)/shard_map/ppermute | solution.py:23
  120.3 9.2 %collective-permute-start.11 = (bf16[256,256]{1,0:T(8,128)(2,1)S(1)}, bf16[256,256]{1,0:T(8,128)(2,1)S(1)}, u32[]{:S(2)}, u32[]{:S(2)}) collective-permute-start(bf16[256,256]{1,0:T(8,128)(2,1)S(1)} %slice.30), channel_id=1, source_target_pairs={{0,2},{1,3},{2,0},{3,1},{4,6},{5,7},{6,4},{7,5},{8,10},{9,11},{10,... | collective-permute-start | bytes 393224 | tf_op jit(solution)/shard_map/ppermute | solution.py:23
  124.1 11.7 %all-to-all-start.4 = ((bf16[8,64,256]{2,1,0:T(8,128)(2,1)}), bf16[8,64,256]{2,1,0:T(8,128)(2,1)S(1)}, u32[]{:S(2)}, u32[]{:S(2)}) async-start(bf16[8,64,256]{2,1,0:T(8,128)(2,1)} %get-tuple-element.81), calls=%async_computation.4 | async-start | bytes 524288 | tf_op jit(solution)/shard_map/all_to_all | solution.py:33

commit v3 on v2

--- a/solution.py
+++ b/solution.py
@@ -48,13 +48,13 @@
     return total
 
 
-def call(kernel, outs, ins, specs, scratch=(), grant=VMEM_GRANT):
+def call(kernel, outs, ins, specs, scratch=(), grant=VMEM_GRANT, out_specs=None):
     outs = [jax.ShapeDtypeStruct(shape, dtype) for shape, dtype in outs]
     return pl.pallas_call(
         kernel,
         out_shape=outs,
         in_specs=specs,
-        out_specs=[IN_VMEM] * len(outs),
+        out_specs=out_specs or [IN_VMEM] * len(outs),
         scratch_shapes=list(scratch),
         compiler_params=pltpu.CompilerParams(vmem_limit_bytes=grant),
     )(*ins)
@@ -180,20 +180,31 @@
 
 
 def turn(got_shift, product_of, slot_shift, width):
-    def kernel(me_ref, got_ref, base_ref, mix_ref, local_ref, maps_ref, own_ref, slots_ref):
+    def kernel(me_ref, got_ref, base_ref, mix_ref, local_ref, maps_ref, own_ref, slots_ref, held, sem):
         me = me_ref[0]
         total = base_ref[...]
         for k in (1, 2, 3):
             total = total + product_of(got_ref[(me >> got_shift & 3) ^ k], mix_ref[k - 1])
         node = total.astype(BF16)
-        own = times_t(node, parts(maps_ref)[0]) + local_ref[...].astype(F32)
-        own = own.astype(BF16)
-        own_ref[...] = own
+        held[...] = node
         place, half = me >> slot_shift & (1 << width) - 1, 1 << width - 1
         near = place & half
-        for k in range(half):
-            slots_ref[near | k] = own
-            slots_ref[(near ^ half) | k] = node
+        far = [
+            pltpu.make_async_copy(held, slots_ref.at[(near ^ half) | k], sem.at[k])
+            for k in range(half)
+        ]
+        for copy in far:
+            copy.start()
+        own = times_t(node, parts(maps_ref)[0]) + local_ref[...].astype(F32)
+        own_ref[...] = own.astype(BF16)
+        beside = [
+            pltpu.make_async_copy(own_ref, slots_ref.at[near | k], sem.at[half + k])
+            for k in range(half)
+        ]
+        for copy in beside:
+            copy.start()
+        for copy in far + beside:
+            copy.wait()
 
     return kernel
 
@@ -364,6 +375,8 @@
             [(block, BF16), ((1 << width, *block), BF16)],
             [me, got, base, mix, local[level], transfer],
             [IN_SMEM] + [IN_VMEM] * 5,
+            [pltpu.VMEM(block, BF16), pltpu.SemaphoreType.DMA((1 << width,))],
+            out_specs=[IN_VMEM, IN_HBM],
         )
 
     def prepare_down(far, own, level):

time: 138 us -> 138 us (level)
  no operation moved by 1% of the time
where the time goes in v3:
time: 138 us; the launch traced here: 137 us
  starting transfers between devices  80.7 us (58%)
  waiting for transfers between devices  36.3 us (26%)
  Pallas kernels  15 us (11%)
  matrix products  3.92 us (3%)
    ppermute x13, starting transfers between devices, swap(): return lax.ppermute(block, AXIS, route)  58.6 us
    all_to_all x5, starting transfers between devices, exchange(): return lax.all_to_all(slots, AXIS, 0, 0, axis_index_groups=groups)  22.2 us
    all_to_all x5, waiting for transfers between devices, exchange(): return lax.all_to_all(slots, AXIS, 0, 0, axis_index_groups=groups)  19.7 us
    ppermute x13, waiting for transfers between devices, swap(): return lax.ppermute(block, AXIS, route)  16.6 us
    pallas_call x16, Pallas kernels, call(): pl.pallas_call(kernel, out_shape=outs, in_specs=specs, out_specs=out_spec...  15 us
    dot_general x19, matrix products, times(): return jnp.dot(values, matrix, preferred_element_type=F32)  3.92 us
  transfers between devices with their start and end apart: 18, of which 8 were waited for; matrix products, arithmetic and copies ran while one was open for 2% of the time, Pallas kernels for 8%

profile of v3, /device:TPU:1, one launch (start us, length us, event | category | flops | bytes accessed | tf_op | source)
XLA Modules:
  0.0 137.4 jit_solution(156661047986194007)
XLA Ops:
  0.0 1.3 convolution_convert_fusion
  1.3 8.7 %collective-permute-start = (bf16[64,256]{1,0:T(8,128)(2,1)S(1)}, bf16[64,256]{1,0:T(8,128)(2,1)S(1)}, u32[]{:S(2)}, u32[]{:S(2)}) collective-permute-start(bf16[64,256]{1,0:T(8,128)(2,1)S(1)} %convolution_convert_fusion), channel_id=1, source_target_pairs={{0,1},{1,0},{2,3},{3,2},{4,5},{5,4},{6,7},{7,6},{8,9},{9,8},{10,11... | collective-permute-start | bytes 98312 | tf_op jit(solution)/shard_map/ppermute | solution.py:23
  11.4 1.9 %collective-permute-start.1 = (bf16[64,256]{1,0:T(8,128)(2,1)S(1)}, bf16[64,256]{1,0:T(8,128)(2,1)S(1)}, u32[]{:S(2)}, u32[]{:S(2)}) collective-permute-start(bf16[64,256]{1,0:T(8,128)(2,1)S(1)} %fusion), channel_id=1, source_target_pairs={{0,2},{1,3},{2,0},{3,1},{4,6},{5,7},{6,4},{7,5},{8,10},{9,11},{10,... | collective-permute-start | bytes 98312 | tf_op jit(solution)/shard_map/ppermute | solution.py:23
  13.4 2.6 %collective-permute-done.1 = bf16[64,256]{1,0:T(8,128)(2,1)S(1)} collective-permute-done((bf16[64,256]{1,0:T(8,128)(2,1)S(1)}, bf16[64,256]{1,0:T(8,128)(2,1)S(1)}, u32[]{:S(2)}, u32[]{:S(2)}) %collective-permute-start.1) | collective-permute-done | bytes 32800 | tf_op jit(solution)/shard_map/ppermute | solution.py:23
  16.2 1.9 %collective-permute-start.2 = (bf16[64,256]{1,0:T(8,128)(2,1)S(1)}, bf16[64,256]{1,0:T(8,128)(2,1)S(1)}, u32[]{:S(2)}, u32[]{:S(2)}) collective-permute-start(bf16[64,256]{1,0:T(8,128)(2,1)S(1)} %fusion.1), channel_id=1, source_target_pairs={{0,4},{1,5},{2,6},{3,7},{4,0},{5,1},{6,2},{7,3},{8,12},{9,13},{10,... | collective-permute-start | bytes 98312 | tf_op jit(solution)/shard_map/ppermute | solution.py:23
  18.2 4.1 %collective-permute-done.2.other_ref = bf16[64,256]{1,0:T(8,128)(2,1)S(1)} collective-permute-done((bf16[64,256]{1,0:T(8,128)(2,1)S(1)}, bf16[64,256]{1,0:T(8,128)(2,1)S(1)}, u32[]{:S(2)}, u32[]{:S(2)}) %collective-permute-start.2) | collective-permute-done | bytes 32800 | tf_op jit(solution)/shard_map/ppermute | solution.py:23
  23.3 3.3 %all-to-all-start = ((bf16[4,64,256]{2,1,0:T(8,128)(2,1)}), bf16[4,64,256]{2,1,0:T(8,128)(2,1)S(1)}, u32[]{:S(2)}, u32[]{:S(2)}) async-start(bf16[4,64,256]{2,1,0:T(8,128)(2,1)} %get-tuple-element.50), calls=%async_computation | async-start | bytes 262144 | tf_op jit(solution)/shard_map/all_to_all | solution.py:33
  26.6 4.2 %collective-permute-start.3 = (bf16[512,256]{1,0:T(8,128)(2,1)S(1)}, bf16[512,256]{1,0:T(8,128)(2,1)S(1)}, u32[]{:S(2)}, u32[]{:S(2)}) collective-permute-start(bf16[512,256]{1,0:T(8,128)(2,1)S(1)} %shard_map.55.maps_ref.refs_7_), channel_id=1, source_target_pairs={{0,16},{1,17},{2,18},{3,19},{4,20},{5,21},{6,22},{7,23},{8,24},{9,... | collective-permute-start | bytes 786440 | tf_op jit(solution)/shard_map/ppermute | solution.py:23
  30.8 2.5 %shard_map.68.refs_3_ = f32[64,1024]{1,0:T(8,128)} custom-call(bf16[64,1024]{1,0:T(8,128)(2,1)} %sides_ref, bf16[1024,1024]{1,0:T(8,128)(2,1)} %inverse_ref.1), custom_call_target="tpu_custom_call" | custom-call | tf_op jit(solution)/shard_map/pallas_call | solution.py:53
  33.4 1.9 %collective-permute-start.6 = (bf16[512,256]{1,0:T(8,128)(2,1)S(1)}, bf16[512,256]{1,0:T(8,128)(2,1)S(1)}, u32[]{:S(2)}, u32[]{:S(2)}) collective-permute-start(bf16[512,256]{1,0:T(8,128)(2,1)S(1)} %shard_map.55.maps_ref.refs_7_), channel_id=1, source_target_pairs={{0,256},{1,257},{2,258},{3,259},{4,260},{5,261},{6,262},{7,263},{8... | collective-permute-start | bytes 786440 | tf_op jit(solution)/shard_map/ppermute | solution.py:23
  35.3 8.1 %collective-permute-done.3.far_ref = bf16[512,256]{1,0:T(8,128)(2,1)S(1)} collective-permute-done((bf16[512,256]{1,0:T(8,128)(2,1)S(1)}, bf16[512,256]{1,0:T(8,128)(2,1)S(1)}, u32[]{:S(2)}, u32[]{:S(2)}) %collective-permute-start.3) | collective-permute-done | bytes 262176 | tf_op jit(solution)/shard_map/ppermute | solution.py:23
  44.3 5.6 %collective-permute-start.4 = (bf16[64,256]{1,0:T(8,128)(2,1)S(1)}, bf16[64,256]{1,0:T(8,128)(2,1)S(1)}, u32[]{:S(2)}, u32[]{:S(2)}) collective-permute-start(bf16[64,256]{1,0:T(8,128)(2,1)S(1)} %shard_map.58), channel_id=1, source_target_pairs={{0,32},{1,33},{2,34},{3,35},{4,36},{5,37},{6,38},{7,39},{8,40},{9,... | collective-permute-start | bytes 98312 | tf_op jit(solution)/shard_map/ppermute | solution.py:23
  52.0 1.2 collective-permute-done.4
  53.5 10.1 %collective-permute-start.5 = (bf16[64,256]{1,0:T(8,128)(2,1)S(1)}, bf16[64,256]{1,0:T(8,128)(2,1)S(1)}, u32[]{:S(2)}, u32[]{:S(2)}) collective-permute-start(bf16[64,256]{1,0:T(8,128)(2,1)S(1)} %fusion.2), channel_id=1, source_target_pairs={{0,64},{1,65},{2,66},{3,67},{4,68},{5,69},{6,70},{7,71},{8,72},{9,... | collective-permute-start | bytes 98312 | tf_op jit(solution)/shard_map/ppermute | solution.py:23
  63.7 3.1 %collective-permute-start.7 = (bf16[4,256,256]{2,1,0:T(8,128)(2,1)S(1)}, bf16[4,256,256]{2,1,0:T(8,128)(2,1)S(1)}, u32[]{:S(2)}, u32[]{:S(2)}) collective-permute-start(bf16[4,256,256]{2,1,0:T(8,128)(2,1)S(1)} %shard_map.60.eighth_ref), channel_id=1, source_target_pairs={{0,128},{1,129},{2,130},{3,131},{4,132},{5,133},{6,134},{7,135},{8... | collective-permute-start | bytes 1572872 | tf_op jit(solution)/shard_map/ppermute | solution.py:23
  66.9 3.7 %collective-permute-start.8 = (bf16[256,256]{1,0:T(8,128)(2,1)S(1)}, bf16[256,256]{1,0:T(8,128)(2,1)S(1)}, u32[]{:S(2)}, u32[]{:S(2)}) collective-permute-start(bf16[256,256]{1,0:T(8,128)(2,1)S(1)} %slice.28), channel_id=1, source_target_pairs={{0,32},{1,33},{2,34},{3,35},{4,36},{5,37},{6,38},{7,39},{8,40},{9,... | collective-permute-start | bytes 393224 | tf_op jit(solution)/shard_map/ppermute | solution.py:23
  71.5 3.7 %all-to-all-start.1 = ((bf16[4,64,256]{2,1,0:T(8,128)(2,1)}), bf16[4,64,256]{2,1,0:T(8,128)(2,1)S(1)}, u32[]{:S(2)}, u32[]{:S(2)}) async-start(bf16[4,64,256]{2,1,0:T(8,128)(2,1)} %get-tuple-element.55), calls=%async_computation.1 | async-start | bytes 262144 | tf_op jit(solution)/shard_map/all_to_all | solution.py:33
  76.9 3.8 %all-to-all-done.1.got_ref = bf16[4,64,256]{2,1,0:T(8,128)(2,1)S(1)} async-done(((bf16[4,64,256]{2,1,0:T(8,128)(2,1)}), bf16[4,64,256]{2,1,0:T(8,128)(2,1)S(1)}, u32[]{:S(2)}, u32[]{:S(2)}) %all-to-all-start.1) | async-done | bytes 131104 | tf_op jit(solution)/shard_map/all_to_all | solution.py:33
  80.7 1.0 shard_map.62
  81.8 6.0 %all-to-all-start.2 = ((bf16[4,64,256]{2,1,0:T(8,128)(2,1)}), bf16[4,64,256]{2,1,0:T(8,128)(2,1)S(1)}, u32[]{:S(2)}, u32[]{:S(2)}) async-start(bf16[4,64,256]{2,1,0:T(8,128)(2,1)} %get-tuple-element.64), calls=%async_computation.2 | async-start | bytes 262144 | tf_op jit(solution)/shard_map/all_to_all | solution.py:33
  88.7 11.1 %all-to-all-done.2.got_ref = bf16[4,64,256]{2,1,0:T(8,128)(2,1)S(1)} async-done(((bf16[4,64,256]{2,1,0:T(8,128)(2,1)}), bf16[4,64,256]{2,1,0:T(8,128)(2,1)S(1)}, u32[]{:S(2)}, u32[]{:S(2)}) %all-to-all-start.2) | async-done | bytes 131104 | tf_op jit(solution)/shard_map/all_to_all | solution.py:33
  99.8 1.1 shard_map.65
  100.9 3.9 %all-to-all-start.3 = ((bf16[4,64,256]{2,1,0:T(8,128)(2,1)}), bf16[4,64,256]{2,1,0:T(8,128)(2,1)S(1)}, u32[]{:S(2)}, u32[]{:S(2)}) async-start(bf16[4,64,256]{2,1,0:T(8,128)(2,1)} %get-tuple-element.73), calls=%async_computation.3 | async-start | bytes 262144 | tf_op jit(solution)/shard_map/all_to_all | solution.py:33
  104.9 3.4 %collective-permute-start.9 = (bf16[256,256]{1,0:T(8,128)(2,1)S(1)}, bf16[256,256]{1,0:T(8,128)(2,1)S(1)}, u32[]{:S(2)}, u32[]{:S(2)}) collective-permute-start(bf16[256,256]{1,0:T(8,128)(2,1)S(1)} %slice.30), channel_id=1, source_target_pairs={{0,8},{1,9},{2,10},{3,11},{4,12},{5,13},{6,14},{7,15},{8,0},{9,1},... | collective-permute-start | bytes 393224 | tf_op jit(solution)/shard_map/ppermute | solution.py:23
  108.3 8.7 %collective-permute-start.10 = (bf16[576,256]{1,0:T(8,128)(2,1)S(1)}, bf16[576,256]{1,0:T(8,128)(2,1)S(1)}, u32[]{:S(2)}, u32[]{:S(2)}) collective-permute-start(bf16[576,256]{1,0:T(8,128)(2,1)S(1)} %pad_maximum_fusion), channel_id=1, source_target_pairs={{0,1},{1,0},{2,3},{3,2},{4,5},{5,4},{6,7},{7,6},{8,9},{9,8},{10,11... | collective-permute-start | bytes 884744 | tf_op jit(solution)/shard_map/ppermute | solution.py:23
  117.2 3.1 %collective-permute-start.12 = (bf16[256,256]{1,0:T(8,128)(2,1)S(1)}, bf16[256,256]{1,0:T(8,128)(2,1)S(1)}, u32[]{:S(2)}, u32[]{:S(2)}) collective-permute-start(bf16[256,256]{1,0:T(8,128)(2,1)S(1)} %slice.30), channel_id=1, source_target_pairs={{0,3},{1,2},{2,1},{3,0},{4,7},{5,6},{6,5},{7,4},{8,11},{9,10},{10,... | collective-permute-start | bytes 393224 | tf_op jit(solution)/shard_map/ppermute | solution.py:23
  120.3 2.1 %collective-permute-start.11 = (bf16[256,256]{1,0:T(8,128)(2,1)S(1)}, bf16[256,256]{1,0:T(8,128)(2,1)S(1)}, u32[]{:S(2)}, u32[]{:S(2)}) collective-permute-start(bf16[256,256]{1,0:T(8,128)(2,1)S(1)} %slice.30), channel_id=1, source_target_pairs={{0,2},{1,3},{2,0},{3,1},{4,6},{5,7},{6,4},{7,5},{8,10},{9,11},{10,... | collective-permute-start | bytes 393224 | tf_op jit(solution)/shard_map/ppermute | solution.py:23
  123.0 1.1 shard_map.67
  124.1 5.2 %all-to-all-start.4 = ((bf16[8,64,256]{2,1,0:T(8,128)(2,1)}), bf16[8,64,256]{2,1,0:T(8,128)(2,1)S(1)}, u32[]{:S(2)}, u32[]{:S(2)}) async-start(bf16[8,64,256]{2,1,0:T(8,128)(2,1)} %get-tuple-element.81), calls=%async_computation.4 | async-start | bytes 524288 | tf_op jit(solution)/shard_map/all_to_all | solution.py:33
  129.6 1.5 %shard_map.69 = (f32[64,1024]{1,0:T(8,128)S(1)}, bf16[7,256,256]{2,1,0:T(8,128)(2,1)S(1)}) custom-call(bf16[576,256]{1,0:T(8,128)(2,1)S(1)} %collective-permute-done.10.refs_0_, bf16[256,256]{1,0:T(8,128)(2,1)S(1)} %collective-permute-done.11.refs_1_, bf16[256,256]{1,0:T(8,128)(2,1)S(1)} %collective-permute-done.12.refs_2_, f32[64,1024]{1,0:T(8,128)S(1)} %copy-done.2, ...), custom_call_target="tpu_custom_call" | custom-call | tf_op jit(solution)/shard_map/pallas_call | solution.py:53
  131.1 4.7 %all-to-all-done.4.got_ref = bf16[8,64,256]{2,1,0:T(8,128)(2,1)S(1)} async-done(((bf16[8,64,256]{2,1,0:T(8,128)(2,1)}), bf16[8,64,256]{2,1,0:T(8,128)(2,1)S(1)}, u32[]{:S(2)}, u32[]{:S(2)}) %all-to-all-start.4) | async-done | bytes 262176 | tf_op jit(solution)/shard_map/all_to_all | solution.py:33
  135.9 1.5 %shard_map.70 = bf16[64,1024]{1,0:T(8,128)(2,1)} custom-call(s32[1]{0:T(128)} %bitcast.me_ref, bf16[8,64,256]{2,1,0:T(8,128)(2,1)S(1)} %all-to-all-done.4.got_ref, f32[64,1024]{1,0:T(8,128)S(1)} %get-tuple-element.91.base_ref, bf16[7,256,256]{2,1,0:T(8,128)(2,1)S(1)} %get-tuple-element.92.mix_ref, bf16[1024,256]{1,0:T(8,128)(2,1)S(1)} %copy-done.1), custom_call_target="tpu_custom_call" | custom-call | tf_op jit(solution)/shard_map/pallas_call | solution.py:53
  (51 shorter events, 10.4 us)
Async XLA Ops:
  1.3 9.9 %collective-permute-start = (bf16[64,256]{1,0:T(8,128)(2,1)S(1)}, bf16[64,256]{1,0:T(8,128)(2,1)S(1)}, u32[]{:S(2)}, u32[]{:S(2)}) collective-permute-start(bf16[64,256]{1,0:T(8,128)(2,1)S(1)} %convolution_convert_fusion), channel_id=1, source_target_pairs={{0,1},{1,0},{2,3},{3,2},{4,5},{5,4},{6,7},{7,6},{8,9},{9,8},{10,11... | collective-permute-start | bytes 98312 | tf_op jit(solution)/shard_map/ppermute | solution.py:23
  10.1 1.0 copy-start.3
  11.4 4.7 %collective-permute-start.1 = (bf16[64,256]{1,0:T(8,128)(2,1)S(1)}, bf16[64,256]{1,0:T(8,128)(2,1)S(1)}, u32[]{:S(2)}, u32[]{:S(2)}) collective-permute-start(bf16[64,256]{1,0:T(8,128)(2,1)S(1)} %fusion), channel_id=1, source_target_pairs={{0,2},{1,3},{2,0},{3,1},{4,6},{5,7},{6,4},{7,5},{8,10},{9,11},{10,... | collective-permute-start | bytes 98312 | tf_op jit(solution)/shard_map/ppermute | solution.py:23
  16.2 6.2 %collective-permute-start.2 = (bf16[64,256]{1,0:T(8,128)(2,1)S(1)}, bf16[64,256]{1,0:T(8,128)(2,1)S(1)}, u32[]{:S(2)}, u32[]{:S(2)}) collective-permute-start(bf16[64,256]{1,0:T(8,128)(2,1)S(1)} %fusion.1), channel_id=1, source_target_pairs={{0,4},{1,5},{2,6},{3,7},{4,0},{5,1},{6,2},{7,3},{8,12},{9,13},{10,... | collective-permute-start | bytes 98312 | tf_op jit(solution)/shard_map/ppermute | solution.py:23
  22.3 27.6 %copy-start = (bf16[512,256]{1,0:T(8,128)(2,1)S(1)}, bf16[512,256]{1,0:T(8,128)(2,1)}, u32[]{:S(2)}) copy-start(bf16[512,256]{1,0:T(8,128)(2,1)} %links_ref.5) | copy-start | bytes 786436
  23.3 20.8 %all-to-all-start = ((bf16[4,64,256]{2,1,0:T(8,128)(2,1)}), bf16[4,64,256]{2,1,0:T(8,128)(2,1)S(1)}, u32[]{:S(2)}, u32[]{:S(2)}) async-start(bf16[4,64,256]{2,1,0:T(8,128)(2,1)} %get-tuple-element.50), calls=%async_computation | async-start | bytes 262144 | tf_op jit(solution)/shard_map/all_to_all | solution.py:33
  26.6 16.8 %collective-permute-start.3 = (bf16[512,256]{1,0:T(8,128)(2,1)S(1)}, bf16[512,256]{1,0:T(8,128)(2,1)S(1)}, u32[]{:S(2)}, u32[]{:S(2)}) collective-permute-start(bf16[512,256]{1,0:T(8,128)(2,1)S(1)} %shard_map.55.maps_ref.refs_7_), channel_id=1, source_target_pairs={{0,16},{1,17},{2,18},{3,19},{4,20},{5,21},{6,22},{7,23},{8,24},{9,... | collective-permute-start | bytes 786440 | tf_op jit(solution)/shard_map/ppermute | solution.py:23
  33.4 17.6 %collective-permute-start.6 = (bf16[512,256]{1,0:T(8,128)(2,1)S(1)}, bf16[512,256]{1,0:T(8,128)(2,1)S(1)}, u32[]{:S(2)}, u32[]{:S(2)}) collective-permute-start(bf16[512,256]{1,0:T(8,128)(2,1)S(1)} %shard_map.55.maps_ref.refs_7_), channel_id=1, source_target_pairs={{0,256},{1,257},{2,258},{3,259},{4,260},{5,261},{6,262},{7,263},{8... | collective-permute-start | bytes 786440 | tf_op jit(solution)/shard_map/ppermute | solution.py:23
  44.3 8.9 %collective-permute-start.4 = (bf16[64,256]{1,0:T(8,128)(2,1)S(1)}, bf16[64,256]{1,0:T(8,128)(2,1)S(1)}, u32[]{:S(2)}, u32[]{:S(2)}) collective-permute-start(bf16[64,256]{1,0:T(8,128)(2,1)S(1)} %shard_map.58), channel_id=1, source_target_pairs={{0,32},{1,33},{2,34},{3,35},{4,36},{5,37},{6,38},{7,39},{8,40},{9,... | collective-permute-start | bytes 98312 | tf_op jit(solution)/shard_map/ppermute | solution.py:23
  53.5 17.1 %collective-permute-start.5 = (bf16[64,256]{1,0:T(8,128)(2,1)S(1)}, bf16[64,256]{1,0:T(8,128)(2,1)S(1)}, u32[]{:S(2)}, u32[]{:S(2)}) collective-permute-start(bf16[64,256]{1,0:T(8,128)(2,1)S(1)} %fusion.2), channel_id=1, source_target_pairs={{0,64},{1,65},{2,66},{3,67},{4,68},{5,69},{6,70},{7,71},{8,72},{9,... | collective-permute-start | bytes 98312 | tf_op jit(solution)/shard_map/ppermute | solution.py:23
  63.7 12.4 %collective-permute-start.7 = (bf16[4,256,256]{2,1,0:T(8,128)(2,1)S(1)}, bf16[4,256,256]{2,1,0:T(8,128)(2,1)S(1)}, u32[]{:S(2)}, u32[]{:S(2)}) collective-permute-start(bf16[4,256,256]{2,1,0:T(8,128)(2,1)S(1)} %shard_map.60.eighth_ref), channel_id=1, source_target_pairs={{0,128},{1,129},{2,130},{3,131},{4,132},{5,133},{6,134},{7,135},{8... | collective-permute-start | bytes 1572872 | tf_op jit(solution)/shard_map/ppermute | solution.py:23
  66.9 21.1 %collective-permute-start.8 = (bf16[256,256]{1,0:T(8,128)(2,1)S(1)}, bf16[256,256]{1,0:T(8,128)(2,1)S(1)}, u32[]{:S(2)}, u32[]{:S(2)}) collective-permute-start(bf16[256,256]{1,0:T(8,128)(2,1)S(1)} %slice.28), channel_id=1, source_target_pairs={{0,32},{1,33},{2,34},{3,35},{4,36},{5,37},{6,38},{7,39},{8,40},{9,... | collective-permute-start | bytes 393224 | tf_op jit(solution)/shard_map/ppermute | solution.py:23
  71.5 9.2 %all-to-all-start.1 = ((bf16[4,64,256]{2,1,0:T(8,128)(2,1)}), bf16[4,64,256]{2,1,0:T(8,128)(2,1)S(1)}, u32[]{:S(2)}, u32[]{:S(2)}) async-start(bf16[4,64,256]{2,1,0:T(8,128)(2,1)} %get-tuple-element.55), calls=%async_computation.1 | async-start | bytes 262144 | tf_op jit(solution)/shard_map/all_to_all | solution.py:33
  81.8 18.1 %all-to-all-start.2 = ((bf16[4,64,256]{2,1,0:T(8,128)(2,1)}), bf16[4,64,256]{2,1,0:T(8,128)(2,1)S(1)}, u32[]{:S(2)}, u32[]{:S(2)}) async-start(bf16[4,64,256]{2,1,0:T(8,128)(2,1)} %get-tuple-element.64), calls=%async_computation.2 | async-start | bytes 262144 | tf_op jit(solution)/shard_map/all_to_all | solution.py:33
  99.8 29.8 %copy-start.1 = (bf16[1024,256]{1,0:T(8,128)(2,1)S(1)}, bf16[1024,256]{1,0:T(8,128)(2,1)}, u32[]{:S(2)}) copy-start(bf16[1024,256]{1,0:T(8,128)(2,1)} %basis_ref.1) | copy-start | bytes 1572868
  99.8 29.8 %copy-start.2 = (f32[64,1024]{1,0:T(8,128)S(1)}, f32[64,1024]{1,0:T(8,128)}, u32[]{:S(2)}) copy-start(f32[64,1024]{1,0:T(8,128)} %shard_map.68.refs_3_) | copy-start | bytes 786436
  100.9 22.1 %all-to-all-start.3 = ((bf16[4,64,256]{2,1,0:T(8,128)(2,1)}), bf16[4,64,256]{2,1,0:T(8,128)(2,1)S(1)}, u32[]{:S(2)}, u32[]{:S(2)}) async-start(bf16[4,64,256]{2,1,0:T(8,128)(2,1)} %get-tuple-element.73), calls=%async_computation.3 | async-start | bytes 262144 | tf_op jit(solution)/shard_map/all_to_all | solution.py:33
  104.9 17.5 %collective-permute-start.9 = (bf16[256,256]{1,0:T(8,128)(2,1)S(1)}, bf16[256,256]{1,0:T(8,128)(2,1)S(1)}, u32[]{:S(2)}, u32[]{:S(2)}) collective-permute-start(bf16[256,256]{1,0:T(8,128)(2,1)S(1)} %slice.30), channel_id=1, source_target_pairs={{0,8},{1,9},{2,10},{3,11},{4,12},{5,13},{6,14},{7,15},{8,0},{9,1},... | collective-permute-start | bytes 393224 | tf_op jit(solution)/shard_map/ppermute | solution.py:23
  108.3 21.2 %collective-permute-start.10 = (bf16[576,256]{1,0:T(8,128)(2,1)S(1)}, bf16[576,256]{1,0:T(8,128)(2,1)S(1)}, u32[]{:S(2)}, u32[]{:S(2)}) collective-permute-start(bf16[576,256]{1,0:T(8,128)(2,1)S(1)} %pad_maximum_fusion), channel_id=1, source_target_pairs={{0,1},{1,0},{2,3},{3,2},{4,5},{5,4},{6,7},{7,6},{8,9},{9,8},{10,11... | collective-permute-start | bytes 884744 | tf_op jit(solution)/shard_map/ppermute | solution.py:23
  117.2 12.3 %collective-permute-start.12 = (bf16[256,256]{1,0:T(8,128)(2,1)S(1)}, bf16[256,256]{1,0:T(8,128)(2,1)S(1)}, u32[]{:S(2)}, u32[]{:S(2)}) collective-permute-start(bf16[256,256]{1,0:T(8,128)(2,1)S(1)} %slice.30), channel_id=1, source_target_pairs={{0,3},{1,2},{2,1},{3,0},{4,7},{5,6},{6,5},{7,4},{8,11},{9,10},{10,... | collective-permute-start | bytes 393224 | tf_op jit(solution)/shard_map/ppermute | solution.py:23
  120.3 9.2 %collective-permute-start.11 = (bf16[256,256]{1,0:T(8,128)(2,1)S(1)}, bf16[256,256]{1,0:T(8,128)(2,1)S(1)}, u32[]{:S(2)}, u32[]{:S(2)}) collective-permute-start(bf16[256,256]{1,0:T(8,128)(2,1)S(1)} %slice.30), channel_id=1, source_target_pairs={{0,2},{1,3},{2,0},{3,1},{4,6},{5,7},{6,4},{7,5},{8,10},{9,11},{10,... | collective-permute-start | bytes 393224 | tf_op jit(solution)/shard_map/ppermute | solution.py:23
  124.1 11.7 %all-to-all-start.4 = ((bf16[8,64,256]{2,1,0:T(8,128)(2,1)}), bf16[8,64,256]{2,1,0:T(8,128)(2,1)S(1)}, u32[]{:S(2)}, u32[]{:S(2)}) async-start(bf16[8,64,256]{2,1,0:T(8,128)(2,1)} %get-tuple-element.81), calls=%async_computation.4 | async-start | bytes 524288 | tf_op jit(solution)/shard_map/all_to_all | solution.py:33
